TPU v7x, 32 devices: a whole 2x2x4 slice. The times are simulated.
32 devices in a mesh: row: 4 (over x, core), col: 2 (over y), date: 4 (over z).
Axes of the slice: x: 2, y: 2, z: 4, core: 2. Of those that a mesh axis runs over, the one named last changes fastest.
Arguments:
- slc: bfloat16 [2, 48, 24, 512], P(None, 'date', 'row', 'col'), may hold values from -6 to 6
- pairs: int32 [32, 2], P('date'), may hold values from 0 to 47, as said below
- target: float32 [2, 32, 12, 128], P(None, 'date', 'row', 'col'), may hold values from -4 to 4
- w_lift: bfloat16 [2, 3, 3, 64], replicated, may hold values from -1.5 to 1.5
- b_lift: bfloat16 [2, 64], replicated, may hold values from -2 to 2
- w_mid: bfloat16 [2, 3, 3, 64, 64], replicated, may hold values from -0.1875 to 0.1875
- b_mid: bfloat16 [2, 64], replicated, may hold values from -2 to 2
- w_proj: bfloat16 [2, 3, 3, 64], replicated, may hold values from -0.1875 to 0.1875
Outputs:
- denoised: float32 [2, 32, 12, 128], P(None, 'date', 'row', 'col')
- grad_lift: float32 [2, 3, 3, 64], replicated
- grad_lift_bias: float32 [2, 64], replicated
- grad_mid: float32 [2, 3, 3, 64, 64], replicated
- grad_mid_bias: float32 [2, 64], replicated
- grad_proj: float32 [2, 3, 3, 64], replicated
Inputs may be any that keep to these rules, and one draw needn't show every extreme that they name: `pairs`: row p belongs to date index p // 8, which holds dates d * 12 to (d + 1) * 12 - 1; its earlier date lies there, and its later date is later by 1 to 24 dates. Row 0 is (0, 24).
All inputs are finite; a program needn't handle non-finite values.
Results may differ from a plain program's by a relative error of at most 0.00065.
The roundings to bfloat16 on the way count: a program that leaves them out, or rounds other values in their place, can miss the bound.
Values may be sent and summed in bfloat16 or wider, within the bound.
A program may use at most 64 MiB of HBM per device.

v0:
```python
import math

import jax
import jax.numpy as jnp
from jax import lax
from jax.sharding import PartitionSpec as P

LR = 2
LC = 4


def extended(block, sides, width):
    for axis, dim in sides:
        count = lax.axis_size(axis)
        forward = [(i, i + 1) for i in range(count - 1)]
        backward = [(target, source) for source, target in forward]
        low = lax.ppermute(
            lax.slice_in_dim(block, block.shape[dim] - width, None, axis=dim), axis, forward
        )
        high = lax.ppermute(lax.slice_in_dim(block, 0, width, axis=dim), axis, backward)
        block = jnp.concatenate([low, block, high], axis=dim)
    return block


def from_behind(block, axis, distance):
    devices = range(lax.axis_size(axis))
    route = [(i - distance, i) for i in devices if i - distance in devices]
    return lax.ppermute(block, axis, route)


def real_block(weights):
    real_part = weights[0]
    imag_part = weights[1]
    upper = jnp.concatenate([real_part, imag_part], axis=-1)
    lower = jnp.concatenate([-imag_part, real_part], axis=-1)
    return jnp.concatenate([upper, lower], axis=-2)


def fold_grads(gram, inner):
    outer = gram.shape[-1] // 2
    real_part = gram[:, :, :inner, :outer] + gram[:, :, inner:, outer:]
    imag_part = gram[:, :, :inner, outer:] - gram[:, :, inner:, :outer]
    return jnp.stack([real_part, imag_part])


def deep_rim(field):
    return extended(field, (("row", 2), ("col", 3)), 3)


def field_rim(field):
    return extended(field, (("row", 2), ("col", 3)), 1)


def grad_rim(hidden):
    return extended(hidden, (("row", 1), ("col", 2)), 1)


def tap_sum(padded_in, kernel, form, offset, on_field):
    height = padded_in.shape[2] - 2 if on_field else padded_in.shape[1] - 2
    breadth = padded_in.shape[3] - 2 if on_field else padded_in.shape[2] - 2
    summed = 0.0
    for row_tap in range(3):
        for col_tap in range(3):
            row_at = 2 - row_tap if offset else row_tap
            col_at = 2 - col_tap if offset else col_tap
            if on_field:
                window = padded_in[:, :, row_at : row_at + height, col_at : col_at + breadth]
            else:
                window = padded_in[:, row_at : row_at + height, col_at : col_at + breadth, :]
            summed = summed + jnp.einsum(
                form, window, kernel[row_tap, col_tap], preferred_element_type=jnp.float32
            )
    return summed


def tap_gram(padded_in, grad_out, form, on_field):
    height = padded_in.shape[2] - 2 if on_field else padded_in.shape[1] - 2
    breadth = padded_in.shape[3] - 2 if on_field else padded_in.shape[2] - 2
    grams = []
    for row_tap in range(3):
        for col_tap in range(3):
            if on_field:
                window = padded_in[:, :, row_tap : row_tap + height, col_tap : col_tap + breadth]
            else:
                window = padded_in[:, row_tap : row_tap + height, col_tap : col_tap + breadth, :]
            grams.append(jnp.einsum(form, window, grad_out, preferred_element_type=jnp.float32))
    stacked = jnp.stack(grams)
    return stacked.reshape((3, 3) + stacked.shape[1:])


def make_looks(slab_pool, local_pairs, look_rows, look_cols):
    slab_span = slab_pool.shape[1]
    choose = (
        local_pairs[:, :, None] == jnp.arange(slab_span, dtype=jnp.int32)[None, None, :]
    ).astype(jnp.bfloat16)
    picked = jnp.einsum("pqk,zkrc->zqprc", choose, slab_pool, preferred_element_type=jnp.float32)
    real_part = picked[0, 0] * picked[0, 1] + picked[1, 0] * picked[1, 1]
    imag_part = picked[1, 0] * picked[0, 1] - picked[0, 0] * picked[1, 1]
    product = jnp.stack([real_part, imag_part])
    count = product.shape[1]
    height = product.shape[2] // look_rows
    breadth = product.shape[3] // look_cols
    return (
        product.reshape(2, count, height, look_rows, breadth, look_cols)
        .mean(axis=(3, 5))
        .astype(jnp.bfloat16)
    )


def inside_mask(first_row, row_count, total_rows, first_col, col_count, total_cols):
    row_spot = first_row + jnp.arange(row_count, dtype=jnp.int32)
    col_spot = first_col + jnp.arange(col_count, dtype=jnp.int32)
    row_good = (row_spot >= 0) & (row_spot < total_rows)
    col_good = (col_spot >= 0) & (col_spot < total_cols)
    return (row_good[:, None] & col_good[None, :])[None, :, :, None]


def local(slc, pairs, target, w_lift, b_lift, w_mid, b_mid, w_proj):
    dates_dev = slc.shape[1]
    date_start = lax.axis_index("date") * dates_dev
    following = []
    carried = slc
    for repeat in range(2):
        carried = from_behind(carried, "date", -1)
        following.append(carried)
    slab_pool = jnp.concatenate([slc] + following, axis=1)
    looks = make_looks(slab_pool, pairs - date_start, LR, LC)
    channels = w_mid.shape[-1]
    lift_block = real_block(w_lift[:, :, :, None, :])
    mid_block = real_block(w_mid)
    proj_block = real_block(w_proj[..., None])
    lift_bias = b_lift.reshape(2 * channels).astype(jnp.float32)
    mid_bias = b_mid.reshape(2 * channels).astype(jnp.float32)
    tile_rows = looks.shape[2]
    tile_cols = looks.shape[3]
    pair_total = looks.shape[1] * lax.axis_size("date")
    looked_rows = tile_rows * lax.axis_size("row")
    looked_cols = tile_cols * lax.axis_size("col")
    loss_scale = 1.0 / math.sqrt(2.0 * pair_total * looked_rows * looked_cols)
    row_first = lax.axis_index("row") * tile_rows
    col_first = lax.axis_index("col") * tile_cols
    looks_deep = deep_rim(looks)
    looks_pad = looks_deep[:, :, 2:-2, 2:-2]
    pre1 = tap_sum(looks_deep, lift_block, "zprc,zo->prco", 0, True) + lift_bias
    outer_mask = inside_mask(
        row_first - 2, tile_rows + 4, looked_rows, col_first - 2, tile_cols + 4, looked_cols
    )
    hidden1_wide = jnp.where(outer_mask, jnp.maximum(pre1, 0.0), 0.0).astype(jnp.bfloat16)
    hidden1_pad = hidden1_wide[:, 1:-1, 1:-1, :]
    hidden1 = hidden1_wide[:, 2:-2, 2:-2, :]
    pre2 = tap_sum(hidden1_wide, mid_block, "prci,io->prco", 0, False) + mid_bias
    inner_mask = inside_mask(
        row_first - 1, tile_rows + 2, looked_rows, col_first - 1, tile_cols + 2, looked_cols
    )
    hidden2_pad = jnp.where(inner_mask, jnp.maximum(pre2, 0.0), 0.0).astype(jnp.bfloat16)
    hidden2 = hidden2_pad[:, 1:-1, 1:-1, :]
    noise = tap_sum(hidden2_pad, proj_block, "prci,iz->zprc", 0, False)
    denoised = looks.astype(jnp.float32) - noise
    d_noise = ((target - denoised) * loss_scale).astype(jnp.bfloat16)
    d_hidden2 = tap_sum(field_rim(d_noise), proj_block, "zprc,iz->prci", 2, True)
    d_pre2 = jnp.where(hidden2 > 0, d_hidden2, 0.0).astype(jnp.bfloat16)
    gram_proj = tap_gram(hidden2_pad, d_noise, "prci,zprc->iz", False)
    d_hidden1 = tap_sum(grad_rim(d_pre2), mid_block, "prco,io->prci", 2, False)
    gram_mid = tap_gram(hidden1_pad, d_pre2, "prci,prco->io", False)
    mid_bias_grad = jnp.sum(d_pre2.astype(jnp.float32), axis=(0, 1, 2))
    d_pre1 = jnp.where(hidden1 > 0, d_hidden1, 0.0).astype(jnp.bfloat16)
    gram_lift = tap_gram(looks_pad, d_pre1, "zprc,prco->zo", True)
    lift_bias_grad = jnp.sum(d_pre1.astype(jnp.float32), axis=(0, 1, 2))
    gram_lift, lift_bias_grad, gram_mid, mid_bias_grad, gram_proj = lax.psum(
        (gram_lift, lift_bias_grad, gram_mid, mid_bias_grad, gram_proj), ("row", "col", "date")
    )
    grad_lift = fold_grads(gram_lift, 1)[:, :, :, 0, :]
    grad_mid = fold_grads(gram_mid, channels)
    grad_proj = fold_grads(gram_proj, channels)[..., 0]
    return (
        denoised,
        grad_lift,
        lift_bias_grad.reshape(2, channels),
        grad_mid,
        mid_bias_grad.reshape(2, channels),
        grad_proj,
    )


def solution(mesh):
    in_specs = (
        P(None, "date", "row", "col"),
        P("date", None),
        P(None, "date", "row", "col"),
        P(),
        P(),
        P(),
        P(),
        P(),
    )
    out_specs = (P(None, "date", "row", "col"), P(), P(), P(), P(), P())
    return jax.shard_map(local, mesh=mesh, in_specs=in_specs, out_specs=out_specs, check_vma=False)
```

profile of v0, /device:TPU:1, one launch (start us, length us, event | category | flops | bytes accessed | tf_op | source)
XLA Modules:
  0.0 226.1 jit_solution(1273168140837796031)
XLA Ops:
  7.2 0.9 copy.61
  8.1 1.3 collective-permute-start
  10.9 1.0 slice_bitcast_fusion
  11.9 0.9 fusion.183
  15.2 1.3 collective-permute-start.1
  16.7 5.7 %collective-permute-done.1 = bf16[2,12,6,256]{3,1,2,0:T(8,128)(2,1)S(1)} collective-permute-done((bf16[2,12,6,256]{3,1,2,0:T(8,128)(2,1)S(1)}, bf16[2,12,6,256]{3,1,2,0:T(8,128)(2,1)S(1)}, u32[]{:S(2)}, u32[]{:S(2)}) %collective-permute-start.1) | collective-permute-done | bytes 73760 | tf_op jit(solution)/shard_map/ppermute | solution.py:28
  23.2 0.9 maximum_reduce_fusion
  24.2 4.5 %collective-permute-start.2 = (bf16[2,8,3,64]{3,0,2,1:T(2,128)(2,1)S(1)}, bf16[2,8,3,64]{3,0,2,1:T(2,128)(2,1)S(1)}, u32[]{:S(2)}, u32[]{:S(2)}) collective-permute-start(bf16[2,8,3,64]{3,0,2,1:T(2,128)(2,1)S(1)} %multiply_convert_fusion), channel_id=1, source_target_pairs={{0,8},{8,16},{16,24},{1,9},{9,17},{17,25},{2,10},{10,18},{18,26},{... | collective-permute-start | bytes 18440 | tf_op jit(solution)/shard_map/ppermute | solution.py:17
  28.7 1.9 collective-permute-start.3
  30.7 3.0 %collective-permute-done.3 = bf16[2,8,3,64]{3,0,2,1:T(2,128)(2,1)S(1)} collective-permute-done((bf16[2,8,3,64]{3,0,2,1:T(2,128)(2,1)S(1)}, bf16[2,8,3,64]{3,0,2,1:T(2,128)(2,1)S(1)}, u32[]{:S(2)}, u32[]{:S(2)}) %collective-permute-start.3) | collective-permute-done | bytes 6176 | tf_op jit(solution)/shard_map/ppermute | solution.py:20
  33.9 3.1 %collective-permute-start.4 = (bf16[2,8,9,3]{3,0,2,1:T(2,128)(2,1)S(1)}, bf16[2,8,9,3]{3,0,2,1:T(2,128)(2,1)S(1)}, u32[]{:S(2)}, u32[]{:S(2)}) collective-permute-start(bf16[2,8,9,3]{3,0,2,1:T(2,128)(2,1)S(1)} %get-tuple-element.48), channel_id=1, source_target_pairs={{0,4},{1,5},{2,6},{3,7},{8,12},{9,13},{10,14},{11,15},{16,20},{17,... | collective-permute-start | bytes 2600 | tf_op jit(solution)/shard_map/ppermute | solution.py:17
  37.0 1.5 collective-permute-start.5
  38.8 2.9 %collective-permute-done.5 = bf16[2,8,9,3]{3,0,2,1:T(2,128)(2,1)S(1)} collective-permute-done((bf16[2,8,9,3]{3,0,2,1:T(2,128)(2,1)S(1)}, bf16[2,8,9,3]{3,0,2,1:T(2,128)(2,1)S(1)}, u32[]{:S(2)}, u32[]{:S(2)}) %collective-permute-start.5) | collective-permute-done | bytes 896 | tf_op jit(solution)/shard_map/ppermute | solution.py:20
  42.4 1.0 fusion.122
  43.4 1.0 fusion.124
  45.0 1.0 fusion.128
  46.0 1.0 fusion.130
  47.5 1.0 fusion.118
  48.5 1.3 select_convert_fusion
  54.1 0.9 select_convert_fusion.1
  61.5 1.9 collective-permute-start.7
  63.4 3.6 %collective-permute-start.6 = (bf16[2,8,1,64]{3,0,2,1:T(2,128)(2,1)S(1)}, bf16[2,8,1,64]{3,0,2,1:T(2,128)(2,1)S(1)}, u32[]{:S(2)}, u32[]{:S(2)}) collective-permute-start(bf16[2,8,1,64]{3,0,2,1:T(2,128)(2,1)S(1)} %get-tuple-element.54), channel_id=1, source_target_pairs={{0,8},{8,16},{16,24},{1,9},{9,17},{17,25},{2,10},{10,18},{18,26},{... | collective-permute-start | bytes 6152 | tf_op jit(solution)/shard_map/ppermute | solution.py:17
  68.0 1.3 collective-permute-start.8
  69.3 4.0 %collective-permute-start.9 = (bf16[2,8,5,1]{3,0,2,1:T(2,128)(2,1)S(1)}, bf16[2,8,5,1]{3,0,2,1:T(2,128)(2,1)S(1)}, u32[]{:S(2)}, u32[]{:S(2)}) collective-permute-start(bf16[2,8,5,1]{3,0,2,1:T(2,128)(2,1)S(1)} %get-tuple-element.53), channel_id=1, source_target_pairs={{0,4},{1,5},{2,6},{3,7},{8,12},{9,13},{10,14},{11,15},{16,20},{17,... | collective-permute-start | bytes 488 | tf_op jit(solution)/shard_map/ppermute | solution.py:17
  77.3 1.9 collective-permute-start.11
  79.2 5.2 %collective-permute-start.10 = (bf16[8,1,64,128]{3,2,1,0:T(8,128)(2,1)S(1)}, bf16[8,1,64,128]{3,2,1,0:T(8,128)(2,1)S(1)}, u32[]{:S(2)}, u32[]{:S(2)}) collective-permute-start(bf16[8,1,64,128]{3,2,1,0:T(8,128)(2,1)S(1)} %get-tuple-element.40), channel_id=1, source_target_pairs={{0,8},{8,16},{16,24},{1,9},{9,17},{17,25},{2,10},{10,18},{18,26},{... | collective-permute-start | bytes 393224 | tf_op jit(solution)/shard_map/ppermute | solution.py:17
  88.2 1.3 collective-permute-start.12
  89.5 4.0 %collective-permute-start.13 = (bf16[8,5,1,128]{3,2,1,0:T(2,128)(2,1)S(1)}, bf16[8,5,1,128]{3,2,1,0:T(2,128)(2,1)S(1)}, u32[]{:S(2)}, u32[]{:S(2)}) collective-permute-start(bf16[8,5,1,128]{3,2,1,0:T(2,128)(2,1)S(1)} %get-tuple-element.37), channel_id=1, source_target_pairs={{0,4},{1,5},{2,6},{3,7},{8,12},{9,13},{10,14},{11,15},{16,20},{17,... | collective-permute-start | bytes 30728 | tf_op jit(solution)/shard_map/ppermute | solution.py:17
  99.3 41.4 %all-reduce = (f32[3,3,2,128]{3,2,1,0:T(2,128)S(1)}, f32[2,64]{1,0:T(2,128)}, f32[2,64]{1,0:T(2,128)}, f32[3,3,128,2]{2,3,1,0:T(2,128)S(1)}) all-reduce(f32[3,3,2,128]{3,2,1,0:T(2,128)S(1)} %bitcast.522, f32[2,64]{1,0:T(2,128)S(1)} %reshape.258, ...), channel_id=1, replica_groups=mesh['row'=4,'col'=2,'date'=4] {'row','col','date'}, use_global_device_ids=true, to_apply=%region_1.2 | all-reduce | flops 4864 | bytes 38912 | tf_op jit(solution)/shard_map/psum | solution.py:169
  142.1 74.8 %all-reduce.3.cloned.1.call-done = f32[3,3,128,128]{3,2,1,0:T(8,128)} async-done(((f32[3,3,128,128]{3,2,1,0:T(8,128)}), f32[3,3,128,128]{3,2,1,0:T(8,128)}) %all-reduce.3.cloned.1.call-update) | async-done | bytes 589840 | tf_op jit(solution)/shard_map/psum | solution.py:169
  216.9 1.5 fusion.108
  218.4 0.9 pad_maximum_fusion.1
  (126 shorter events, 33.5 us)
Async XLA Ops:
  7.2 209.7 %all-reduce.3.cloned.1.call-start = ((), (), s32[]{:S(2)}) async-start(), calls=%async_computation | async-start | bytes 1179648 | tf_op jit(solution)/shard_map/psum | solution.py:169
  8.1 7.1 %collective-permute-start = (bf16[2,12,6,256]{3,1,2,0:T(8,128)(2,1)S(1)}, bf16[2,12,6,256]{3,1,2,0:T(8,128)(2,1)S(1)}, u32[]{:S(2)}, u32[]{:S(2)}) collective-permute-start(bf16[2,12,6,256]{3,1,2,0:T(8,128)(2,1)S(1)} %copy.61), channel_id=1, source_target_pairs={{1,0},{2,1},{3,2},{5,4},{6,5},{7,6},{9,8},{10,9},{11,10},{13,12},{... | collective-permute-start | bytes 221192 | tf_op jit(solution)/shard_map/ppermute | solution.py:28
  15.2 7.1 %collective-permute-start.1 = (bf16[2,12,6,256]{3,1,2,0:T(8,128)(2,1)S(1)}, bf16[2,12,6,256]{3,1,2,0:T(8,128)(2,1)S(1)}, u32[]{:S(2)}, u32[]{:S(2)}) collective-permute-start(bf16[2,12,6,256]{3,1,2,0:T(8,128)(2,1)S(1)} %collective-permute-done), channel_id=1, source_target_pairs={{1,0},{2,1},{3,2},{5,4},{6,5},{7,6},{9,8},{10,9},{11,10},{13,12},{... | collective-permute-start | bytes 221192 | tf_op jit(solution)/shard_map/ppermute | solution.py:28
  22.9 15.7 %copy-start.2 = (bf16[2,64]{1,0:T(2,128)(2,1)S(1)}, bf16[2,64]{1,0:T(2,128)(2,1)}, u32[]{:S(2)}) copy-start(bf16[2,64]{1,0:T(2,128)(2,1)} %param.12) | copy-start | bytes 772
  22.9 15.8 %copy-start.3 = (bf16[2,64]{1,0:T(2,128)(2,1)S(1)}, bf16[2,64]{1,0:T(2,128)(2,1)}, u32[]{:S(2)}) copy-start(bf16[2,64]{1,0:T(2,128)(2,1)} %param.14) | copy-start | bytes 772
  24.2 6.5 %collective-permute-start.2 = (bf16[2,8,3,64]{3,0,2,1:T(2,128)(2,1)S(1)}, bf16[2,8,3,64]{3,0,2,1:T(2,128)(2,1)S(1)}, u32[]{:S(2)}, u32[]{:S(2)}) collective-permute-start(bf16[2,8,3,64]{3,0,2,1:T(2,128)(2,1)S(1)} %multiply_convert_fusion), channel_id=1, source_target_pairs={{0,8},{8,16},{16,24},{1,9},{9,17},{17,25},{2,10},{10,18},{18,26},{... | collective-permute-start | bytes 18440 | tf_op jit(solution)/shard_map/ppermute | solution.py:17
  28.7 5.0 %collective-permute-start.3 = (bf16[2,8,3,64]{3,0,2,1:T(2,128)(2,1)S(1)}, bf16[2,8,3,64]{3,0,2,1:T(2,128)(2,1)S(1)}, u32[]{:S(2)}, u32[]{:S(2)}) collective-permute-start(bf16[2,8,3,64]{3,0,2,1:T(2,128)(2,1)S(1)} %multiply_convert_fusion), channel_id=1, source_target_pairs={{8,0},{16,8},{24,16},{9,1},{17,9},{25,17},{10,2},{18,10},{26,18},{... | collective-permute-start | bytes 18440 | tf_op jit(solution)/shard_map/ppermute | solution.py:20
  33.9 4.9 %collective-permute-start.4 = (bf16[2,8,9,3]{3,0,2,1:T(2,128)(2,1)S(1)}, bf16[2,8,9,3]{3,0,2,1:T(2,128)(2,1)S(1)}, u32[]{:S(2)}, u32[]{:S(2)}) collective-permute-start(bf16[2,8,9,3]{3,0,2,1:T(2,128)(2,1)S(1)} %get-tuple-element.48), channel_id=1, source_target_pairs={{0,4},{1,5},{2,6},{3,7},{8,12},{9,13},{10,14},{11,15},{16,20},{17,... | collective-permute-start | bytes 2600 | tf_op jit(solution)/shard_map/ppermute | solution.py:17
  37.0 4.7 %collective-permute-start.5 = (bf16[2,8,9,3]{3,0,2,1:T(2,128)(2,1)S(1)}, bf16[2,8,9,3]{3,0,2,1:T(2,128)(2,1)S(1)}, u32[]{:S(2)}, u32[]{:S(2)}) collective-permute-start(bf16[2,8,9,3]{3,0,2,1:T(2,128)(2,1)S(1)} %get-tuple-element.49), channel_id=1, source_target_pairs={{4,0},{5,1},{6,2},{7,3},{12,8},{13,9},{14,10},{15,11},{20,16},{21,... | collective-permute-start | bytes 2600 | tf_op jit(solution)/shard_map/ppermute | solution.py:20
  56.3 2.1 copy-start.1
  61.5 6.4 %collective-permute-start.7 = (bf16[2,8,1,64]{3,0,2,1:T(2,128)(2,1)S(1)}, bf16[2,8,1,64]{3,0,2,1:T(2,128)(2,1)S(1)}, u32[]{:S(2)}, u32[]{:S(2)}) collective-permute-start(bf16[2,8,1,64]{3,0,2,1:T(2,128)(2,1)S(1)} %get-tuple-element.55), channel_id=1, source_target_pairs={{8,0},{16,8},{24,16},{9,1},{17,9},{25,17},{10,2},{18,10},{26,18},{... | collective-permute-start | bytes 6152 | tf_op jit(solution)/shard_map/ppermute | solution.py:20
  63.4 4.5 %collective-permute-start.6 = (bf16[2,8,1,64]{3,0,2,1:T(2,128)(2,1)S(1)}, bf16[2,8,1,64]{3,0,2,1:T(2,128)(2,1)S(1)}, u32[]{:S(2)}, u32[]{:S(2)}) collective-permute-start(bf16[2,8,1,64]{3,0,2,1:T(2,128)(2,1)S(1)} %get-tuple-element.54), channel_id=1, source_target_pairs={{0,8},{8,16},{16,24},{1,9},{9,17},{17,25},{2,10},{10,18},{18,26},{... | collective-permute-start | bytes 6152 | tf_op jit(solution)/shard_map/ppermute | solution.py:17
  68.0 5.9 %collective-permute-start.8 = (bf16[2,8,5,1]{3,0,2,1:T(2,128)(2,1)S(1)}, bf16[2,8,5,1]{3,0,2,1:T(2,128)(2,1)S(1)}, u32[]{:S(2)}, u32[]{:S(2)}) collective-permute-start(bf16[2,8,5,1]{3,0,2,1:T(2,128)(2,1)S(1)} %get-tuple-element.52), channel_id=1, source_target_pairs={{4,0},{5,1},{6,2},{7,3},{12,8},{13,9},{14,10},{15,11},{20,16},{21,... | collective-permute-start | bytes 488 | tf_op jit(solution)/shard_map/ppermute | solution.py:20
  69.3 4.9 %collective-permute-start.9 = (bf16[2,8,5,1]{3,0,2,1:T(2,128)(2,1)S(1)}, bf16[2,8,5,1]{3,0,2,1:T(2,128)(2,1)S(1)}, u32[]{:S(2)}, u32[]{:S(2)}) collective-permute-start(bf16[2,8,5,1]{3,0,2,1:T(2,128)(2,1)S(1)} %get-tuple-element.53), channel_id=1, source_target_pairs={{0,4},{1,5},{2,6},{3,7},{8,12},{9,13},{10,14},{11,15},{16,20},{17,... | collective-permute-start | bytes 488 | tf_op jit(solution)/shard_map/ppermute | solution.py:17
  77.3 10.8 %collective-permute-start.11 = (bf16[8,1,64,128]{3,2,1,0:T(8,128)(2,1)S(1)}, bf16[8,1,64,128]{3,2,1,0:T(8,128)(2,1)S(1)}, u32[]{:S(2)}, u32[]{:S(2)}) collective-permute-start(bf16[8,1,64,128]{3,2,1,0:T(8,128)(2,1)S(1)} %get-tuple-element.41), channel_id=1, source_target_pairs={{8,0},{16,8},{24,16},{9,1},{17,9},{25,17},{10,2},{18,10},{26,18},{... | collective-permute-start | bytes 393224 | tf_op jit(solution)/shard_map/ppermute | solution.py:20
  79.2 8.9 %collective-permute-start.10 = (bf16[8,1,64,128]{3,2,1,0:T(8,128)(2,1)S(1)}, bf16[8,1,64,128]{3,2,1,0:T(8,128)(2,1)S(1)}, u32[]{:S(2)}, u32[]{:S(2)}) collective-permute-start(bf16[8,1,64,128]{3,2,1,0:T(8,128)(2,1)S(1)} %get-tuple-element.40), channel_id=1, source_target_pairs={{0,8},{8,16},{16,24},{1,9},{9,17},{17,25},{2,10},{10,18},{18,26},{... | collective-permute-start | bytes 393224 | tf_op jit(solution)/shard_map/ppermute | solution.py:17
  87.0 0.8 copy-start
  88.2 5.8 %collective-permute-start.12 = (bf16[8,5,1,128]{3,2,1,0:T(2,128)(2,1)S(1)}, bf16[8,5,1,128]{3,2,1,0:T(2,128)(2,1)S(1)}, u32[]{:S(2)}, u32[]{:S(2)}) collective-permute-start(bf16[8,5,1,128]{3,2,1,0:T(2,128)(2,1)S(1)} %get-tuple-element.36), channel_id=1, source_target_pairs={{4,0},{5,1},{6,2},{7,3},{12,8},{13,9},{14,10},{15,11},{20,16},{21,... | collective-permute-start | bytes 30728 | tf_op jit(solution)/shard_map/ppermute | solution.py:20
  89.5 4.9 %collective-permute-start.13 = (bf16[8,5,1,128]{3,2,1,0:T(2,128)(2,1)S(1)}, bf16[8,5,1,128]{3,2,1,0:T(2,128)(2,1)S(1)}, u32[]{:S(2)}, u32[]{:S(2)}) collective-permute-start(bf16[8,5,1,128]{3,2,1,0:T(2,128)(2,1)S(1)} %get-tuple-element.37), channel_id=1, source_target_pairs={{0,4},{1,5},{2,6},{3,7},{8,12},{9,13},{10,14},{11,15},{16,20},{17,... | collective-permute-start | bytes 30728 | tf_op jit(solution)/shard_map/ppermute | solution.py:17
Sparse Core Ops, SparseCore 0:
  88.0 128.8 all-reduce.2
where the time goes:
time: 227 us; the launch traced here: 226 us
  waiting for transfers between devices  87 us (38%)
  blocking collectives  41.4 us (18%)
  starting transfers between devices  36.9 us (16%)
  matrix products  30.8 us (14%)
  between operations  14.7 us (6%)
  other arithmetic  9.31 us (4%)
  local copies, waits for them, and re-layouts  6.08 us (3%)
    psum x1, waiting for transfers between devices, local(): lax.psum((gram_lift, lift_bias_grad, gram_mid, mid_bias_grad, gram_proj),...  74.8 us
    psum x1, blocking collectives, local(): lax.psum((gram_lift, lift_bias_grad, gram_mid, mid_bias_grad, gram_proj),...  41.4 us
    ppermute x6, starting transfers between devices, extended(): lax.ppermute(lax.slice_in_dim(block, block.shape[dim] - width, None, axis...  24.5 us
    dot_general x45, matrix products, tap_sum(): jnp.einsum(form, window, kernel[row_tap, col_tap], preferred_element_type...  23 us
    ppermute x6, starting transfers between devices, extended(): lax.ppermute(lax.slice_in_dim(block, 0, width, axis=dim), axis, backward)  9.82 us
    dot_general x27, matrix products, tap_gram(): jnp.einsum(form, window, grad_out, preferred_element_type=jnp.float32)  7.63 us
    ppermute x6, waiting for transfers between devices, extended(): lax.ppermute(lax.slice_in_dim(block, 0, width, axis=dim), axis, backward)  5.94 us
    ppermute x2, waiting for transfers between devices, from_behind(): return lax.ppermute(block, axis, route)  5.67 us
  transfers between devices with their start and end apart: 15, of which 6 were waited for; matrix products, arithmetic and copies ran while one was open for 8% of the time, Pallas kernels for 0%

commit v1 on v0

v1 whole, which is shorter than its diff:
```python
import functools
import math

import jax
import jax.numpy as jnp
from jax import lax
from jax.experimental import pallas as pl
from jax.experimental.pallas import tpu as pltpu
from jax.sharding import PartitionSpec as P

MESH = pl.DeviceIdType.MESH

LR = 2
LC = 4


def real_block(weights):
    real_part = weights[0]
    imag_part = weights[1]
    upper = jnp.concatenate([real_part, imag_part], axis=-1)
    lower = jnp.concatenate([-imag_part, real_part], axis=-1)
    return jnp.concatenate([upper, lower], axis=-2)


def mm(a, b):
    return jnp.dot(a, b, preferred_element_type=jnp.float32)


def mm_t(a, b):
    return lax.dot_general(a, b, (((1,), (1,)), ((), ())), preferred_element_type=jnp.float32)


def step_kernel(
    dims, scale,
    slc_ref, pick_ref, avg_ref, tgt_ref, w1_ref, wf_ref, bm_ref, wp_ref, wpb_ref, wb_ref,
    den_ref, o_ref,
    pool, look_f, look_s, look_r, tgt_r, fld, tfld, i3a, i3b, h2s, tsum, dn3, dnm3, dp2m, dp1, outs, x_ref,
    plane_in, date_in, slab_sem, look_sem, tgt_sem, den_sem, plane_sem, date_sem, gather_sem,
):
    n_row, n_col, n_date, pp, tr, tc = dims
    r, c, d = lax.axis_index("row"), lax.axis_index("col"), lax.axis_index("date")
    n_plane = n_row * n_col
    me = r * n_col + c
    rows = n_row * tr
    gap = rows + 1
    nb = gap * pp
    n = nb * 128
    base = (128 - tc) // 2
    pairs = pp * n_row
    f32, bf16 = jnp.float32, jnp.bfloat16

    def plane_peer(k):
        peer = lax.rem(me + k, n_plane)
        return peer, (lax.div(peer, n_col), lax.rem(peer, n_col), d)

    def date_peer(k):
        return (r, c, lax.rem(d + k, n_date))

    def remote(src, dst, sems, at, where):
        copy = pltpu.make_async_remote_copy(
            src_ref=src, dst_ref=dst, send_sem=sems.at[0, at], recv_sem=sems.at[1, at],
            device_id=where, device_id_type=MESH,
        )
        copy.start()
        return copy

    barrier = pltpu.get_barrier_semaphore()
    for k in range(1, n_plane):
        pl.semaphore_signal(barrier, inc=1, device_id=plane_peer(k)[1], device_id_type=MESH)
    for k in range(1, n_date):
        pl.semaphore_signal(barrier, inc=1, device_id=date_peer(k), device_id_type=MESH)
    pl.semaphore_wait(barrier, n_plane + n_date - 2)

    sent = []
    slabs = [remote(slc_ref, pool.at[k - 1], slab_sem, k, date_peer(n_date - k)) for k in (1, 2)]

    def exchange(src, dst, sems):
        copies = []
        for way in range(3):
            col = lax.rem(c + (0, 1, n_col - 1)[way], n_col)
            for o in range(n_row):
                k = lax.rem(r + o, n_row)
                at = way * n_row + o
                if way == 0 and o == 0:
                    copy = pltpu.make_async_copy(src.at[k], dst.at[0, r], sems.at[0, at])
                    copy.start()
                    copies.append((copy, True))
                else:
                    copies.append((remote(src.at[k], dst.at[way, r], sems, at, (k, col, d)), False))
        return copies

    tgt_copies = exchange(tgt_ref, tgt_r, tgt_sem)
    for ref in (fld, tfld, dn3, dnm3, tsum):
        ref[...] = jnp.zeros_like(ref)
    edge = jnp.zeros((i3a.shape[0], 128), bf16)
    for ref in (i3a, i3b):
        ref[:, 0:128] = edge
        ref[:, (nb + 1) * 128 : (nb + 2) * 128] = edge
    x_ref[...] = jnp.zeros_like(x_ref)
    lane = lax.broadcasted_iota(jnp.int32, (1, 128), 1)
    spot = c * tc + lane - base
    inside = (spot >= 0) & (spot < n_col * tc)
    own = (lane >= base) & (lane < base + tc)
    for copy in slabs:
        copy.wait_recv()
    sent += slabs

    depth = slc_ref.shape[0]
    picked = (
        mm(pick_ref[:, :depth], slc_ref[...])
        + mm(pick_ref[:, depth : 2 * depth], pool[0])
        + mm(pick_ref[:, 2 * depth :], pool[1])
    )
    parts = slc_ref.shape[1] // (LR * tr)
    halves = tc * LC // parts
    sides = []
    for h in range(halves):
        at = [picked[q * pairs : (q + 1) * pairs] for q in (h, halves + h, 2 * halves + h, 3 * halves + h)]
        a0, a1, b0, b1 = at
        rowsum = []
        for prod in (a0 * b0 + a1 * b1, a1 * b0 - a0 * b1):
            for t in range(tr):
                rowsum.append(
                    sum(prod[:, (t * LR + q) * parts : (t * LR + q + 1) * parts] for q in range(LR))
                )
        sides.append(jnp.concatenate(rowsum, axis=0))
    looked = jnp.dot(
        jnp.concatenate(sides, axis=1), avg_ref[...],
        precision=lax.Precision.HIGHEST, preferred_element_type=f32,
    )
    look_f[...] = jnp.zeros_like(look_f)
    for k in range(n_row):
        for q in range(2 * tr):
            look_f[k, q * pp : (q + 1) * pp, :] = looked[q * pairs + k * pp : q * pairs + (k + 1) * pp]
    look_s[...] = look_f[...].astype(bf16)
    look_copies = exchange(look_s, look_r, look_sem)

    def settle(copies):
        for copy, near in copies:
            if near:
                copy.wait()
            else:
                copy.wait_recv()
                sent.append(copy)

    def assemble(ref, s):
        mid = pltpu.roll(ref[0, s].astype(f32), base, 1)
        low = pltpu.roll(ref[1, s].astype(f32), (base - tc) % 128, 1)
        high = pltpu.roll(ref[2, s].astype(f32), base + tc, 1)
        joined = jnp.where(own, mid, jnp.where(lane < base, low, high))
        near = (lane >= base - 5) & (lane < base + tc + 5)
        return jnp.where(inside & near, joined, 0.0)

    settle(tgt_copies)
    for s in range(n_row):
        block = assemble(tgt_r, s)
        for z in range(2):
            for t in range(tr):
                for p in range(pp):
                    i = (z * tr + t) * pp + p
                    b = p * gap + s * tr + t
                    tfld[z : z + 1, b * 128 : (b + 1) * 128] = block[i : i + 1]
    settle(look_copies)
    for s in range(n_row):
        block = assemble(look_r, s)
        for u, turned in enumerate((pltpu.roll(block, 1, 1), block, pltpu.roll(block, 127, 1))):
            for z in range(2):
                for t in range(tr):
                    for p in range(pp):
                        i = (z * tr + t) * pp + p
                        b = p * gap + s * tr + t + 1
                        fld[2 * u + z : 2 * u + z + 1, b * 128 : (b + 1) * 128] = turned[i : i + 1]
    fld[6:7, :] = jnp.ones((1, (nb + 2) * 128), f32)

    def taps(ref, at, width):
        three = [ref[:, pl.ds(pl.multiple_of(at + t * 128, 128), width)] for t in range(3)]
        return jnp.concatenate(three + [jnp.zeros((8, width), f32)], axis=0).astype(bf16)

    def turned_store(ref, value, at):
        for u, turn in enumerate((1, 0, 127)):
            for q in range(2):
                piece = value[:, q * 128 : (q + 1) * 128]
                if turn:
                    piece = pltpu.roll(piece, turn, 1)
                ref[u * 128 : (u + 1) * 128, pl.ds(pl.multiple_of(at + (q + 1) * 128, 128), 128)] = (
                    piece.astype(bf16)
                )

    def good(b):
        one = [inside & (lax.rem(b + q, gap) != gap - 1) for q in range(2)]
        return jnp.concatenate(one, axis=1)

    own2 = jnp.concatenate([own, own], axis=1)

    def rounded(value):
        return value.astype(bf16).astype(f32)

    def lift(i, carry):
        at = pl.multiple_of(i * 256, 256)
        pre1 = mm(w1_ref[...], taps(fld, at, 256))
        turned_store(i3a, rounded(jnp.where(good(2 * i), jnp.maximum(pre1, 0.0), 0.0)), at)
        return carry

    lax.fori_loop(0, nb // 2, lift, 0)

    def conv(w_ref, ref, at):
        total = 0.0
        for t in range(3):
            total = total + mm(w_ref[t], ref[:, pl.ds(pl.multiple_of(at + t * 128, 128), 256)])
        return total

    def mid(i, carry):
        at = pl.multiple_of(i * 256, 256)
        pre2 = conv(wf_ref, i3a, at) + bm_ref[...]
        h2 = jnp.where(good(2 * i), jnp.maximum(pre2, 0.0), 0.0).astype(bf16)
        h2s[:, pl.ds(at, 256)] = h2
        tsum[:, pl.ds(pl.multiple_of(at + 128, 128), 256)] = mm(wp_ref[...], h2)
        return carry

    lax.fori_loop(0, nb // 2, mid, 0)

    six = sum(tsum[8 * t : 8 * t + 8, t * 128 : t * 128 + n] for t in range(3))
    noise = pltpu.roll(six, 1, 1)[0:2] + six[2:4] + pltpu.roll(six, n - 1, 1)[4:6]
    den = fld[2:4, 128 : 128 + n] - noise
    shifted = pltpu.roll(den, n - base, 1)
    outs[...] = jnp.zeros_like(outs)
    for s in range(n_row):
        for z in range(2):
            for t in range(tr):
                for p in range(pp):
                    i = (z * tr + t) * pp + p
                    b = p * gap + s * tr + t
                    outs[s, i : i + 1, :] = shifted[z : z + 1, b * 128 : (b + 1) * 128]
    den_copies = []
    for o in range(n_row):
        k = lax.rem(r + o, n_row)
        if o == 0:
            copy = pltpu.make_async_copy(outs.at[k], den_ref.at[r], den_sem.at[0, o])
            copy.start()
            den_copies.append((copy, True))
        else:
            den_copies.append((remote(outs.at[k], den_ref.at[r], den_sem, o, (k, c, d)), False))
    dn = rounded((tfld[0:2, :] - den) * scale)
    rowok = [jnp.full((1, 128), b % gap != gap - 1) for b in range(nb)]
    mask = jnp.concatenate([inside & ok for ok in rowok], axis=1)
    own_all = jnp.concatenate([own & ok for ok in rowok], axis=1)
    for ref, keep in ((dn3, mask), (dnm3, own_all)):
        kept = jnp.where(keep, dn, 0.0)
        ref[0:2, 128 : 128 + n] = pltpu.roll(kept, 1, 1)
        ref[2:4, 128 : 128 + n] = kept
        ref[4:6, 128 : 128 + n] = pltpu.roll(kept, n - 1, 1)

    def back2(i, carry):
        at = pl.multiple_of(i * 256, 256)
        grad = mm(wpb_ref[...], taps(dn3, at, 256))
        grad = rounded(jnp.where(h2s[:, pl.ds(at, 256)].astype(f32) > 0, grad, 0.0))
        turned_store(i3b, grad, at)
        dp2m[:, pl.ds(at, 256)] = jnp.where(own2, grad, 0.0).astype(bf16)
        return carry

    lax.fori_loop(0, nb // 2, back2, 0)

    def back1(i, carry):
        at = pl.multiple_of(i * 256, 256)
        h1 = i3a[128:256, pl.ds(pl.multiple_of(at + 128, 128), 256)].astype(f32)
        grad = jnp.where((h1 > 0) & own2, conv(wb_ref, i3b, at), 0.0)
        dp1[:, pl.ds(at, 256)] = grad.astype(bf16)
        return carry

    lax.fori_loop(0, nb // 2, back1, 0)

    sign = jnp.where(lane < 64, 1.0, -1.0)
    for t in range(3):
        gram = mm_t(i3a[:, t * 128 : t * 128 + n], dp2m[...])
        for u in range(3):
            upper = gram[u * 128 : u * 128 + 64]
            lower = gram[u * 128 + 64 : u * 128 + 128]
            x_ref[(3 * t + u) * 64 : (3 * t + u) * 64 + 64, :] = upper + sign * pltpu.roll(lower, 64, 1)
    x_ref[576:600, :] = mm_t(taps(fld, 0, n), dp1[...])[0:24]
    x_ref[600:624, :] = mm_t(taps(dnm3, 0, n), h2s[...])[0:24]
    x_ref[624:632, :] = mm_t(jnp.ones((16, n), bf16), dp2m[...])[0:8]

    piece = plane_in.shape[1]

    def slot(ref, k):
        return ref.at[pl.ds(pl.multiple_of(k * piece, 8), piece)]

    scatter = []
    for k in range(1, n_plane):
        peer, where = plane_peer(k)
        scatter.append(remote(slot(x_ref, peer), plane_in.at[k], plane_sem, k, where))
    part = slot(x_ref, me)[...]
    for k, copy in zip(range(1, n_plane), scatter):
        copy.wait_recv()
        part = part + plane_in[k]
    date_in[d] = part
    spread = [remote(date_in.at[d], date_in.at[d], date_sem, k, date_peer(k)) for k in range(1, n_date)]
    for copy in spread:
        copy.wait_recv()
    slot(o_ref, me)[...] = functools.reduce(lambda a, b: a + b, [date_in[k] for k in range(n_date)])
    gather = [
        remote(slot(o_ref, me), slot(o_ref, me), gather_sem, k, plane_peer(k)[1])
        for k in range(1, n_plane)
    ]
    for copy in gather:
        copy.wait_recv()
    settle(den_copies)
    for copy in sent + scatter + spread + gather:
        copy.wait_send()


def local(slc, pairs, target, w_lift, b_lift, w_mid, b_mid, w_proj):
    n_row, n_col, n_date = (lax.axis_size(axis) for axis in ("row", "col", "date"))
    dates, srows, scols = slc.shape[1:]
    count, tr, tc = target.shape[1:]
    ch = w_mid.shape[-1]
    pp = count // n_row
    halves = scols // 128
    bf16, f32 = jnp.bfloat16, jnp.float32
    rows = 2 * tr * pp
    pad_rows = -(-rows // 16) * 16
    packed = slc.reshape(2, dates, srows, halves, 128).transpose(1, 0, 3, 2, 4)
    packed = packed.reshape(dates * 2 * halves, srows * 128)
    index = (pairs - lax.axis_index("date") * dates).T
    kinds = 2 * halves
    want = (index[:, None, :] * kinds + jnp.arange(kinds, dtype=jnp.int32)[None, :, None]).reshape(-1)
    pick = (want[:, None] == jnp.arange(3 * dates * kinds, dtype=jnp.int32)[None, :]).astype(bf16)
    spots = jnp.arange(scols, dtype=jnp.int32)[:, None] // LC
    avg = jnp.where(spots == jnp.arange(128, dtype=jnp.int32)[None, :], 1.0 / (LR * LC), 0.0).astype(f32)
    tgt = target.reshape(2, n_row, pp, tr, tc).transpose(1, 0, 3, 2, 4).reshape(n_row, rows, tc)
    tgt = jnp.pad(tgt, ((0, 0), (0, pad_rows - rows), (0, 128 - tc)))
    lift = real_block(w_lift[:, :, :, None, :])
    lift = jnp.pad(lift.reshape(3, 6, 2 * ch), ((0, 0), (0, 2), (0, 0)))
    lift = lift.at[1, 6].set(b_lift.reshape(2 * ch))
    w1 = jnp.pad(lift.reshape(24, 2 * ch), ((0, 8), (0, 0))).T
    mid = real_block(w_mid)
    wf = mid.reshape(3, 6 * ch, 2 * ch).transpose(0, 2, 1)
    wb = mid[::-1, ::-1].transpose(0, 2, 1, 3).reshape(3, 2 * ch, 6 * ch)
    proj = real_block(w_proj[..., None])

    def tap_rows(kernel):
        kernel = kernel.transpose(0, 1, 3, 2).reshape(3, 6, 2 * ch)
        kernel = jnp.pad(kernel, ((0, 0), (0, 2), (0, 0))).reshape(24, 2 * ch)
        return jnp.pad(kernel, ((0, 8), (0, 0)))

    wp = tap_rows(proj)
    wpb = tap_rows(proj[::-1, ::-1]).T
    bm = b_mid.reshape(2 * ch, 1).astype(f32)
    scale = 1.0 / math.sqrt(2.0 * count * n_date * tr * n_row * tc * n_col)
    nb = (n_row * tr + 1) * pp
    n, wide = nb * 128, (nb + 2) * 128
    n_plane = n_row * n_col
    piece = -(-632 // (8 * n_plane)) * 8
    dma = pltpu.SemaphoreType.DMA
    vmem = pltpu.VMEM
    den, sums = pl.pallas_call(
        functools.partial(step_kernel, (n_row, n_col, n_date, pp, tr, tc), scale),
        out_shape=(
            jax.ShapeDtypeStruct((n_row, pad_rows, 128), f32),
            jax.ShapeDtypeStruct((n_plane * piece, 128), f32),
        ),
        in_specs=[pl.BlockSpec(memory_space=vmem)] * 10,
        out_specs=(pl.BlockSpec(memory_space=vmem),) * 2,
        scratch_shapes=[
            vmem((2,) + packed.shape, bf16),
            vmem((n_row, pad_rows, 128), f32),
            vmem((n_row, pad_rows, 128), bf16),
            vmem((3, n_row, pad_rows, 128), bf16),
            vmem((3, n_row, pad_rows, 128), f32),
            vmem((8, wide), f32),
            vmem((8, n), f32),
            vmem((6 * ch, wide), bf16),
            vmem((6 * ch, wide), bf16),
            vmem((2 * ch, n), bf16),
            vmem((32, wide), f32),
            vmem((8, wide), f32),
            vmem((8, wide), f32),
            vmem((2 * ch, n), bf16),
            vmem((2 * ch, n), bf16),
            vmem((n_row, pad_rows, 128), f32),
            vmem((n_plane * piece, 128), f32),
            vmem((n_plane, piece, 128), f32),
            vmem((n_date, piece, 128), f32),
            dma((2, 3)),
            dma((2, 3 * n_row)),
            dma((2, 3 * n_row)),
            dma((2, n_row)),
            dma((2, n_plane)),
            dma((2, n_date)),
            dma((2, n_plane)),
        ],
        compiler_params=pltpu.CompilerParams(
            collective_id=0, has_side_effects=True, vmem_limit_bytes=48 * 1024 * 1024
        ),
    )(packed, pick, avg, tgt, w1, wf, bm, wp, wpb, wb)
    denoised = den[:, :rows, :tc].reshape(n_row, 2, tr, pp, tc).transpose(1, 0, 3, 2, 4)
    denoised = denoised.reshape(2, count, tr, tc)
    grad_mid = sums[: 9 * ch].reshape(3, 3, ch, 2, ch).transpose(3, 0, 1, 2, 4)
    g_lift = sums[576:600].reshape(3, 8, 2 * ch)
    lift_bias = g_lift[1, 6]
    g_lift = g_lift[:, :6].reshape(3, 3, 2, 2, ch)
    grad_lift = jnp.stack(
        [g_lift[:, :, 0, 0] + g_lift[:, :, 1, 1], g_lift[:, :, 0, 1] - g_lift[:, :, 1, 0]]
    )
    g_proj = sums[600:624].reshape(3, 8, 2 * ch)[:, :6].reshape(3, 3, 2, 2, ch)[::-1, ::-1]
    grad_proj = jnp.stack(
        [g_proj[:, :, 0, 0] + g_proj[:, :, 1, 1], g_proj[:, :, 1, 0] - g_proj[:, :, 0, 1]]
    )
    return (
        denoised,
        grad_lift,
        lift_bias.reshape(2, ch),
        grad_mid,
        sums[624].reshape(2, ch),
        grad_proj,
    )


def solution(mesh):
    in_specs = (
        P(None, "date", "row", "col"),
        P("date", None),
        P(None, "date", "row", "col"),
        P(),
        P(),
        P(),
        P(),
        P(),
    )
    out_specs = (P(None, "date", "row", "col"), P(), P(), P(), P(), P())
    return jax.shard_map(local, mesh=mesh, in_specs=in_specs, out_specs=out_specs, check_vma=False)
```

time: 227 us -> 62.2 us (0.27)
  waiting for transfers between devices: 87 us -> 0 us
  Pallas kernels: 0 us -> 49.4 us
  blocking collectives: 41.4 us -> 0 us
  starting transfers between devices: 36.9 us -> 0 us
  matrix products: 30.8 us -> 0 us
  between operations: 14.7 us -> 0.91 us
  other arithmetic: 9.31 us -> 1.9 us
  local copies, waits for them, and re-layouts: 6.08 us -> 9.6 us
    psum x1 -> x0, waiting for transfers between devices: 74.8 us -> none  [local(): lax.psum((gram_lift, lift_bias_grad, gram_mid, mid_bias_grad, gram_proj),...]
    pallas_call x0 -> x1, Pallas kernels: none -> 49.4 us  [local(): pl.pallas_call(functools.partial(step_kernel, (n_row, n_col, n_date, pp,...]
    psum x1 -> x0, blocking collectives: 41.4 us -> none  [local(): lax.psum((gram_lift, lift_bias_grad, gram_mid, mid_bias_grad, gram_proj),...]
    ppermute x14 -> x0, starting transfers between devices: 36.9 us -> none  [the longest x6 24.5 us: extended(): lax.ppermute(lax.slice_in_dim(block, block.shape[dim] - width, None, axis...]
    dot_general x73 -> x0, matrix products: 30.8 us -> none  [the longest x45 23 us: tap_sum(): jnp.einsum(form, window, kernel[row_tap, col_tap], preferred_element_type...]
    ppermute x14 -> x0, waiting for transfers between devices: 12.2 us -> none  [the longest x6 5.94 us: extended(): lax.ppermute(lax.slice_in_dim(block, 0, width, axis=dim), axis, backward)]
    squeeze x3 -> x1, local copies, waits for them, and re-layouts: 2.56 us -> 0.02 us  [real_block(): imag_part = weights[1]]
    unnamed x10 -> x20, local copies, waits for them, and re-layouts: 2.33 us -> 4.67 us
  transfers between devices with their start and end apart: 15 -> 0, of which waited for: 6 -> 0; matrix products, arithmetic and copies ran while one was open for 8% -> 0% of each run, Pallas kernels for 0% -> 0%
where the time goes in v1:
time: 62.2 us; the launch traced here: 61.8 us
  Pallas kernels  49.4 us (79%)
  local copies, waits for them, and re-layouts  9.6 us (15%)
  other arithmetic  1.9 us (3%)
  between operations  0.91 us (1%)
    pallas_call x1, Pallas kernels, local(): pl.pallas_call(functools.partial(step_kernel, (n_row, n_col, n_date, pp,...  49.4 us
    unnamed x20, local copies, waits for them, and re-layouts  4.67 us

profile of v1, /device:TPU:1, one launch (start us, length us, event | category | flops | bytes accessed | tf_op | source)
XLA Modules:
  0.0 61.8 jit_solution(16137598380471690661)
XLA Ops:
  0.6 0.7 %copy-done.5 = s32[8,2]{0,1:T(2,128)S(1)} copy-done((s32[8,2]{0,1:T(2,128)S(1)}, s32[8,2]{0,1:T(2,128)}, u32[]{:S(2)}) %copy-start.5) | copy-done | bytes 88
  1.3 0.6 %copy-done.7 = bf16[2,64]{1,0:T(2,128)(2,1)S(1)} copy-done((bf16[2,64]{1,0:T(2,128)(2,1)S(1)}, bf16[2,64]{1,0:T(2,128)(2,1)}, u32[]{:S(2)}) %copy-start.7) | copy-done | bytes 280
  2.0 0.1 reshape.281
  2.1 0.1 add.71
  2.2 0.6 copy-done.3
  2.8 0.1 maximum_maximum_fusion.1
  3.0 0.6 %copy-done.4 = bf16[2,3,3,64]{3,0,2,1:T(2,128)(2,1)S(1)} copy-done((bf16[2,3,3,64]{3,0,2,1:T(2,128)(2,1)S(1)}, bf16[2,3,3,64]{3,0,2,1:T(2,128)(2,1)}, u32[]{:S(2)}) %copy-start.4) | copy-done | bytes 2328
  3.6 0.1 fusion.10
  3.7 0.1 maximum_maximum_fusion.2
  3.9 0.7 %copy-done.2 = f32[2,8,3,64]{3,1,2,0:T(8,128)S(1)} copy-done((f32[2,8,3,64]{3,1,2,0:T(8,128)S(1)}, f32[2,8,3,64]{3,1,2,0:T(8,128)}, u32[]{:S(2)}) %copy-start.2) | copy-done | bytes 12312
  4.6 0.1 copy.54
  4.8 0.1 copy.49
  4.9 0.1 fusion.1.pick_ref
  5.0 0.5 copy-done.6
  5.5 0.1 reshape.297.bm_ref
  5.7 0.1 copy-done.1
  5.9 0.1 fusion.avg_ref
  6.0 0.7 %copy-done = bf16[2,3,3,64,64]{4,3,2,1,0:T(8,128)(2,1)S(1)} copy-done((bf16[2,3,3,64,64]{4,3,2,1,0:T(8,128)(2,1)S(1)}, bf16[2,3,3,64,64]{4,3,2,1,0:T(8,128)(2,1)}, u32[]{:S(2)}) %copy-start) | copy-done | bytes 147480
  6.8 0.2 maximum_maximum_fusion
  7.0 0.2 copy.50
  7.2 0.2 copy.55
  7.5 0.2 copy.57.wb_ref
  7.7 49.4 %shard_map.127 = (f32[4,16,128]{2,1,0:T(8,128)S(1)}, f32[640,128]{1,0:T(8,128)S(1)}) custom-call(bf16[48,768]{1,0:T(8,128)(2,1)S(1)} %bitcast.86, bf16[64,144]{1,0:T(8,128)(2,1)S(1)} %fusion.1.pick_ref, f32[256,128]{1,0:T(8,128)S(1)} %fusion.avg_ref, f32[4,16,128]{2,1,0:T(8,128)S(1)} %pad.27.tgt_ref, bf16[128,32]{1,0:T(8,128)(2,1)S(1)} %get-tuple-element.39.w1_ref, ...), custom_call_target="tpu_custom_call" | custom-call | tf_op jit(solution)/shard_map/pallas_call | solution.py:356
  57.1 0.6 %copy.59 = f32[2,4,2,3,64]{4,2,1,3,0:T(2,128)} copy(f32[2,4,2,3,64]{4,1,2,3,0:T(4,128)S(1)} %bitcast.92) | data formatting | bytes 24576 | tf_op jit(solution)/shard_map/transpose | solution.py:396
  57.7 0.6 %reshape_squeeze.7 = f32[2,64]{1,0:T(2,128)} reshape(f32[128]{0:T(128)S(1)} %slice_reduce_fusion.1) | data formatting | bytes 1024 | tf_op jit(solution)/shard_map/reshape;squeeze | solution.py:414
  58.4 0.6 %reshape_squeeze.6 = f32[2,64]{1,0:T(2,128)} reshape(f32[128]{0:T(128)S(1)} %slice_reduce_fusion) | data formatting | bytes 1024 | tf_op jit(solution)/shard_map/reshape;squeeze | solution.py:412
  59.1 0.1 reshape.295
  59.2 0.6 pad_maximum_fusion.1
  59.8 0.1 reshape.292
  59.9 0.6 pad_maximum_fusion
  60.6 0.4 reshape.293
  60.9 0.9 %copy.82 = f32[3,3,64,2,64]{4,2,1,0,3:T(8,128)} copy(f32[3,3,64,2,64]{4,3,2,1,0:T(2,128)S(1)} %reshape.293) | data formatting | bytes 589824 | tf_op jit(solution)/shard_map/reshape | solution.py:398
  (49 shorter events, 0.6 us)
Async XLA Ops:
  0.6 0.7 %copy-start.5 = (s32[8,2]{0,1:T(2,128)S(1)}, s32[8,2]{0,1:T(2,128)}, u32[]{:S(2)}) copy-start(s32[8,2]{0,1:T(2,128)} %param.11) | copy-start | bytes 196
  1.3 0.7 %copy-start.7 = (bf16[2,64]{1,0:T(2,128)(2,1)S(1)}, bf16[2,64]{1,0:T(2,128)(2,1)}, u32[]{:S(2)}) copy-start(bf16[2,64]{1,0:T(2,128)(2,1)} %param.14) | copy-start | bytes 772
  2.1 0.7 %copy-start.3 = (bf16[2,3,3,64]{3,0,2,1:T(2,128)(2,1)S(1)}, bf16[2,3,3,64]{3,0,2,1:T(2,128)(2,1)}, u32[]{:S(2)}) copy-start(bf16[2,3,3,64]{3,0,2,1:T(2,128)(2,1)} %param.13) | copy-start | bytes 6916
  2.9 0.7 %copy-start.4 = (bf16[2,3,3,64]{3,0,2,1:T(2,128)(2,1)S(1)}, bf16[2,3,3,64]{3,0,2,1:T(2,128)(2,1)}, u32[]{:S(2)}) copy-start(bf16[2,3,3,64]{3,0,2,1:T(2,128)(2,1)} %param.17) | copy-start | bytes 6916
  3.9 0.7 %copy-start.2 = (f32[2,8,3,64]{3,1,2,0:T(8,128)S(1)}, f32[2,8,3,64]{3,1,2,0:T(8,128)}, u32[]{:S(2)}) copy-start(f32[2,8,3,64]{3,1,2,0:T(8,128)} %param.12) | copy-start | bytes 36868
  4.9 0.7 %copy-start.6 = (bf16[2,64]{1,0:T(2,128)(2,1)S(1)}, bf16[2,64]{1,0:T(2,128)(2,1)}, u32[]{:S(2)}) copy-start(bf16[2,64]{1,0:T(2,128)(2,1)} %param.16) | copy-start | bytes 772
  4.9 0.9 %copy-start.1 = (bf16[2,12,6,256]{3,0,2,1:T(2,128)(2,1)S(1)}, bf16[2,12,6,256]{3,0,2,1:T(2,128)(2,1)}, u32[]{:S(2)}) copy-start(bf16[2,12,6,256]{3,0,2,1:T(2,128)(2,1)} %param.10) | copy-start | bytes 221188
  5.8 1.0 %copy-start = (bf16[2,3,3,64,64]{4,3,2,1,0:T(8,128)(2,1)S(1)}, bf16[2,3,3,64,64]{4,3,2,1,0:T(8,128)(2,1)}, u32[]{:S(2)}) copy-start(bf16[2,3,3,64,64]{4,3,2,1,0:T(8,128)(2,1)} %param.15) | copy-start | bytes 442372

commit v2 on v1

--- a/solution.py
+++ b/solution.py
@@ -33,9 +33,9 @@
 def step_kernel(
     dims, scale,
     slc_ref, pick_ref, avg_ref, tgt_ref, w1_ref, wf_ref, bm_ref, wp_ref, wpb_ref, wb_ref,
-    den_ref, o_ref,
+    den_ref, o_ref, small_ref,
     pool, look_f, look_s, look_r, tgt_r, fld, tfld, i3a, i3b, h2s, tsum, dn3, dnm3, dp2m, dp1, outs, x_ref,
-    plane_in, date_in, slab_sem, look_sem, tgt_sem, den_sem, plane_sem, date_sem, gather_sem,
+    plane_in, date_in, small_in, small_date, small_sem, small_date_sem, slab_sem, look_sem, tgt_sem, den_sem, plane_sem, date_sem, gather_sem,
 ):
     n_row, n_col, n_date, pp, tr, tc = dims
     r, c, d = lax.axis_index("row"), lax.axis_index("col"), lax.axis_index("date")
@@ -201,7 +201,7 @@
         turned_store(i3a, rounded(jnp.where(good(2 * i), jnp.maximum(pre1, 0.0), 0.0)), at)
         return carry
 
-    lax.fori_loop(0, nb // 2, lift, 0)
+    lax.fori_loop(0, nb // 2, lift, 0, unroll=True)
 
     def conv(w_ref, ref, at):
         total = 0.0
@@ -217,7 +217,7 @@
         tsum[:, pl.ds(pl.multiple_of(at + 128, 128), 256)] = mm(wp_ref[...], h2)
         return carry
 
-    lax.fori_loop(0, nb // 2, mid, 0)
+    lax.fori_loop(0, nb // 2, mid, 0, unroll=True)
 
     six = sum(tsum[8 * t : 8 * t + 8, t * 128 : t * 128 + n] for t in range(3))
     noise = pltpu.roll(six, 1, 1)[0:2] + six[2:4] + pltpu.roll(six, n - 1, 1)[4:6]
@@ -258,16 +258,7 @@
         dp2m[:, pl.ds(at, 256)] = jnp.where(own2, grad, 0.0).astype(bf16)
         return carry
 
-    lax.fori_loop(0, nb // 2, back2, 0)
-
-    def back1(i, carry):
-        at = pl.multiple_of(i * 256, 256)
-        h1 = i3a[128:256, pl.ds(pl.multiple_of(at + 128, 128), 256)].astype(f32)
-        grad = jnp.where((h1 > 0) & own2, conv(wb_ref, i3b, at), 0.0)
-        dp1[:, pl.ds(at, 256)] = grad.astype(bf16)
-        return carry
-
-    lax.fori_loop(0, nb // 2, back1, 0)
+    lax.fori_loop(0, nb // 2, back2, 0, unroll=True)
 
     sign = jnp.where(lane < 64, 1.0, -1.0)
     for t in range(3):
@@ -276,9 +267,8 @@
             upper = gram[u * 128 : u * 128 + 64]
             lower = gram[u * 128 + 64 : u * 128 + 128]
             x_ref[(3 * t + u) * 64 : (3 * t + u) * 64 + 64, :] = upper + sign * pltpu.roll(lower, 64, 1)
-    x_ref[576:600, :] = mm_t(taps(fld, 0, n), dp1[...])[0:24]
-    x_ref[600:624, :] = mm_t(taps(dnm3, 0, n), h2s[...])[0:24]
-    x_ref[624:632, :] = mm_t(jnp.ones((16, n), bf16), dp2m[...])[0:8]
+    x_ref[576:600, :] = mm_t(taps(dnm3, 0, n), h2s[...])[0:24]
+    x_ref[600:608, :] = mm_t(jnp.ones((16, n), bf16), dp2m[...])[0:8]
 
     piece = plane_in.shape[1]
 
@@ -289,23 +279,50 @@
     for k in range(1, n_plane):
         peer, where = plane_peer(k)
         scatter.append(remote(slot(x_ref, peer), plane_in.at[k], plane_sem, k, where))
+
+    def back1(i, carry):
+        at = pl.multiple_of(i * 256, 256)
+        h1 = i3a[128:256, pl.ds(pl.multiple_of(at + 128, 128), 256)].astype(f32)
+        grad = jnp.where((h1 > 0) & own2, conv(wb_ref, i3b, at), 0.0)
+        dp1[:, pl.ds(at, 256)] = grad.astype(bf16)
+        return carry
+
+    lax.fori_loop(0, nb // 2, back1, 0, unroll=True)
+
+    small_in[me] = mm_t(taps(fld, 0, n), dp1[...])[0:24]
+    small = [
+        remote(small_in.at[me], small_in.at[me], small_sem, k, plane_peer(k)[1]) for k in range(1, n_plane)
+    ]
     part = slot(x_ref, me)[...]
     for k, copy in zip(range(1, n_plane), scatter):
         copy.wait_recv()
         part = part + plane_in[k]
     date_in[d] = part
     spread = [remote(date_in.at[d], date_in.at[d], date_sem, k, date_peer(k)) for k in range(1, n_date)]
+
+    def total(ref, count):
+        return functools.reduce(lambda a, b: a + b, [ref[k] for k in range(count)])
+
+    for copy in small:
+        copy.wait_recv()
+    small_date[d] = total(small_in, n_plane)
+    small_spread = [
+        remote(small_date.at[d], small_date.at[d], small_date_sem, k, date_peer(k)) for k in range(1, n_date)
+    ]
     for copy in spread:
         copy.wait_recv()
-    slot(o_ref, me)[...] = functools.reduce(lambda a, b: a + b, [date_in[k] for k in range(n_date)])
+    slot(o_ref, me)[...] = total(date_in, n_date)
     gather = [
         remote(slot(o_ref, me), slot(o_ref, me), gather_sem, k, plane_peer(k)[1])
         for k in range(1, n_plane)
     ]
+    for copy in small_spread:
+        copy.wait_recv()
+    small_ref[...] = total(small_date, n_date)
+    settle(den_copies)
     for copy in gather:
         copy.wait_recv()
-    settle(den_copies)
-    for copy in sent + scatter + spread + gather:
+    for copy in sent + scatter + small + spread + small_spread + gather:
         copy.wait_send()
 
 
@@ -350,17 +367,18 @@
     nb = (n_row * tr + 1) * pp
     n, wide = nb * 128, (nb + 2) * 128
     n_plane = n_row * n_col
-    piece = -(-632 // (8 * n_plane)) * 8
+    piece = -(-608 // (8 * n_plane)) * 8
     dma = pltpu.SemaphoreType.DMA
     vmem = pltpu.VMEM
-    den, sums = pl.pallas_call(
+    den, sums, small = pl.pallas_call(
         functools.partial(step_kernel, (n_row, n_col, n_date, pp, tr, tc), scale),
         out_shape=(
             jax.ShapeDtypeStruct((n_row, pad_rows, 128), f32),
             jax.ShapeDtypeStruct((n_plane * piece, 128), f32),
+            jax.ShapeDtypeStruct((24, 128), f32),
         ),
         in_specs=[pl.BlockSpec(memory_space=vmem)] * 10,
-        out_specs=(pl.BlockSpec(memory_space=vmem),) * 2,
+        out_specs=(pl.BlockSpec(memory_space=vmem),) * 3,
         scratch_shapes=[
             vmem((2,) + packed.shape, bf16),
             vmem((n_row, pad_rows, 128), f32),
@@ -381,6 +399,10 @@
             vmem((n_plane * piece, 128), f32),
             vmem((n_plane, piece, 128), f32),
             vmem((n_date, piece, 128), f32),
+            vmem((n_plane, 24, 128), f32),
+            vmem((n_date, 24, 128), f32),
+            dma((2, n_plane)),
+            dma((2, n_date)),
             dma((2, 3)),
             dma((2, 3 * n_row)),
             dma((2, 3 * n_row)),
@@ -396,13 +418,13 @@
     denoised = den[:, :rows, :tc].reshape(n_row, 2, tr, pp, tc).transpose(1, 0, 3, 2, 4)
     denoised = denoised.reshape(2, count, tr, tc)
     grad_mid = sums[: 9 * ch].reshape(3, 3, ch, 2, ch).transpose(3, 0, 1, 2, 4)
-    g_lift = sums[576:600].reshape(3, 8, 2 * ch)
+    g_lift = small.reshape(3, 8, 2 * ch)
     lift_bias = g_lift[1, 6]
     g_lift = g_lift[:, :6].reshape(3, 3, 2, 2, ch)
     grad_lift = jnp.stack(
         [g_lift[:, :, 0, 0] + g_lift[:, :, 1, 1], g_lift[:, :, 0, 1] - g_lift[:, :, 1, 0]]
     )
-    g_proj = sums[600:624].reshape(3, 8, 2 * ch)[:, :6].reshape(3, 3, 2, 2, ch)[::-1, ::-1]
+    g_proj = sums[576:600].reshape(3, 8, 2 * ch)[:, :6].reshape(3, 3, 2, 2, ch)[::-1, ::-1]
     grad_proj = jnp.stack(
         [g_proj[:, :, 0, 0] + g_proj[:, :, 1, 1], g_proj[:, :, 1, 0] - g_proj[:, :, 0, 1]]
     )
@@ -411,7 +433,7 @@
         grad_lift,
         lift_bias.reshape(2, ch),
         grad_mid,
-        sums[624].reshape(2, ch),
+        sums[600].reshape(2, ch),
         grad_proj,
     )
 

time: 62.2 us -> 52.8 us (0.85)
  Pallas kernels: 49.4 us -> 40 us
    pallas_call x1, Pallas kernels: 49.4 us -> 40 us  [local(): pl.pallas_call(functools.partial(step_kernel, (n_row, n_col, n_date, pp,...]
where the time goes in v2:
time: 52.8 us; the launch traced here: 52.4 us
  Pallas kernels  40 us (76%)
  local copies, waits for them, and re-layouts  9.6 us (18%)
  other arithmetic  1.9 us (4%)
  between operations  0.91 us (2%)
    pallas_call x1, Pallas kernels, local(): pl.pallas_call(functools.partial(step_kernel, (n_row, n_col, n_date, pp,...  40 us
    unnamed x20, local copies, waits for them, and re-layouts  4.67 us
    reshape x2, local copies, waits for them, and re-layouts, local(): grad_mid = sums[:9 * ch].reshape(3, 3, ch, 2, ch).transpose(3, 0, 1, 2, 4)  1.24 us

profile of v2, /device:TPU:1, one launch (start us, length us, event | category | flops | bytes accessed | tf_op | source)
XLA Modules:
  0.0 52.4 jit_solution(17102242368549504226)
XLA Ops:
  0.6 0.7 %copy-done.5 = s32[8,2]{0,1:T(2,128)S(1)} copy-done((s32[8,2]{0,1:T(2,128)S(1)}, s32[8,2]{0,1:T(2,128)}, u32[]{:S(2)}) %copy-start.5) | copy-done | bytes 88
  1.3 0.6 %copy-done.7 = bf16[2,64]{1,0:T(2,128)(2,1)S(1)} copy-done((bf16[2,64]{1,0:T(2,128)(2,1)S(1)}, bf16[2,64]{1,0:T(2,128)(2,1)}, u32[]{:S(2)}) %copy-start.7) | copy-done | bytes 280
  2.0 0.1 reshape.281
  2.1 0.1 add.71
  2.2 0.6 %copy-done.3 = bf16[2,3,3,64]{3,0,2,1:T(2,128)(2,1)S(1)} copy-done((bf16[2,3,3,64]{3,0,2,1:T(2,128)(2,1)S(1)}, bf16[2,3,3,64]{3,0,2,1:T(2,128)(2,1)}, u32[]{:S(2)}) %copy-start.3) | copy-done | bytes 2328
  2.8 0.1 maximum_maximum_fusion.1
  3.0 0.6 %copy-done.4 = bf16[2,3,3,64]{3,0,2,1:T(2,128)(2,1)S(1)} copy-done((bf16[2,3,3,64]{3,0,2,1:T(2,128)(2,1)S(1)}, bf16[2,3,3,64]{3,0,2,1:T(2,128)(2,1)}, u32[]{:S(2)}) %copy-start.4) | copy-done | bytes 2328
  3.6 0.1 fusion.10
  3.7 0.1 maximum_maximum_fusion.2
  3.9 0.7 %copy-done.2 = f32[2,8,3,64]{3,1,2,0:T(8,128)S(1)} copy-done((f32[2,8,3,64]{3,1,2,0:T(8,128)S(1)}, f32[2,8,3,64]{3,1,2,0:T(8,128)}, u32[]{:S(2)}) %copy-start.2) | copy-done | bytes 12312
  4.6 0.1 copy.54
  4.8 0.1 copy.49
  4.9 0.1 fusion.1.pick_ref
  5.0 0.5 %copy-done.6 = bf16[2,64]{1,0:T(2,128)(2,1)S(1)} copy-done((bf16[2,64]{1,0:T(2,128)(2,1)S(1)}, bf16[2,64]{1,0:T(2,128)(2,1)}, u32[]{:S(2)}) %copy-start.6) | copy-done | bytes 280
  5.5 0.1 reshape.297.bm_ref
  5.7 0.1 copy-done.1
  5.9 0.1 fusion.avg_ref
  6.0 0.7 %copy-done = bf16[2,3,3,64,64]{4,3,2,1,0:T(8,128)(2,1)S(1)} copy-done((bf16[2,3,3,64,64]{4,3,2,1,0:T(8,128)(2,1)S(1)}, bf16[2,3,3,64,64]{4,3,2,1,0:T(8,128)(2,1)}, u32[]{:S(2)}) %copy-start) | copy-done | bytes 147480
  6.8 0.2 maximum_maximum_fusion
  7.0 0.2 copy.50
  7.2 0.2 copy.55
  7.5 0.2 copy.57.wb_ref
  7.7 40.0 %shard_map.127 = (f32[4,16,128]{2,1,0:T(8,128)S(1)}, f32[640,128]{1,0:T(8,128)S(1)}, f32[24,128]{1,0:T(8,128)S(1)}) custom-call(bf16[48,768]{1,0:T(8,128)(2,1)S(1)} %bitcast.85, bf16[64,144]{1,0:T(8,128)(2,1)S(1)} %fusion.1.pick_ref, f32[256,128]{1,0:T(8,128)S(1)} %fusion.avg_ref, f32[4,16,128]{2,1,0:T(8,128)S(1)} %pad.27.tgt_ref, ...), custom_call_target="tpu_custom_call" | custom-call | tf_op jit(solution)/shard_map/pallas_call | solution.py:373
  47.7 0.6 %copy.59 = f32[2,4,2,3,64]{4,2,1,3,0:T(2,128)} copy(f32[2,4,2,3,64]{4,1,2,3,0:T(4,128)S(1)} %bitcast.93) | data formatting | bytes 24576 | tf_op jit(solution)/shard_map/transpose | solution.py:418
  48.4 0.6 %reshape_squeeze.6 = f32[2,64]{1,0:T(2,128)} reshape(f32[128]{0:T(128)S(1)} %slice_reduce_fusion) | data formatting | bytes 1024 | tf_op jit(solution)/shard_map/reshape;squeeze | solution.py:434
  49.1 0.6 %reshape_squeeze.7 = f32[2,64]{1,0:T(2,128)} reshape(f32[128]{0:T(128)S(1)} %slice_reduce_fusion.1) | data formatting | bytes 1024 | tf_op jit(solution)/shard_map/reshape;squeeze | solution.py:436
  49.7 0.1 reshape.295
  49.9 0.6 %pad_maximum_fusion.1 = f32[2,3,3,64]{3,0,2,1:T(2,128)} fusion(f32[1,3,3,64]{3,0,2,1:T(1,128)S(1)} %subtract_bitcast_fusion, f32[1,3,3,64]{3,0,2,1:T(1,128)S(1)} %add_bitcast_fusion), kind=kLoop, calls=%fused_computation.14 | loop fusion | flops 1152 | bytes 9216 | tf_op jit(solution)/shard_map/stack | solution.py:428
  50.5 0.1 reshape.292
  50.6 0.6 %pad_maximum_fusion = f32[2,3,3,64]{3,0,2,1:T(2,128)} fusion(f32[1,3,3,64]{3,0,2,1:T(1,128)S(1)} %fusion.2, f32[1,3,3,64]{3,0,2,1:T(1,128)S(1)} %fusion.4), kind=kLoop, calls=%fused_computation.13 | loop fusion | flops 1152 | bytes 9216 | tf_op jit(solution)/shard_map/stack | solution.py:424
  51.2 0.4 reshape.293
  51.6 0.9 %copy.82 = f32[3,3,64,2,64]{4,2,1,0,3:T(8,128)} copy(f32[3,3,64,2,64]{4,3,2,1,0:T(2,128)S(1)} %reshape.293) | data formatting | bytes 589824 | tf_op jit(solution)/shard_map/reshape | solution.py:420
  (49 shorter events, 0.6 us)
Async XLA Ops:
  0.6 0.7 %copy-start.5 = (s32[8,2]{0,1:T(2,128)S(1)}, s32[8,2]{0,1:T(2,128)}, u32[]{:S(2)}) copy-start(s32[8,2]{0,1:T(2,128)} %param.11) | copy-start | bytes 196
  1.3 0.7 %copy-start.7 = (bf16[2,64]{1,0:T(2,128)(2,1)S(1)}, bf16[2,64]{1,0:T(2,128)(2,1)}, u32[]{:S(2)}) copy-start(bf16[2,64]{1,0:T(2,128)(2,1)} %param.14) | copy-start | bytes 772
  2.1 0.7 %copy-start.3 = (bf16[2,3,3,64]{3,0,2,1:T(2,128)(2,1)S(1)}, bf16[2,3,3,64]{3,0,2,1:T(2,128)(2,1)}, u32[]{:S(2)}) copy-start(bf16[2,3,3,64]{3,0,2,1:T(2,128)(2,1)} %param.13) | copy-start | bytes 6916
  2.9 0.7 %copy-start.4 = (bf16[2,3,3,64]{3,0,2,1:T(2,128)(2,1)S(1)}, bf16[2,3,3,64]{3,0,2,1:T(2,128)(2,1)}, u32[]{:S(2)}) copy-start(bf16[2,3,3,64]{3,0,2,1:T(2,128)(2,1)} %param.17) | copy-start | bytes 6916
  3.9 0.7 %copy-start.2 = (f32[2,8,3,64]{3,1,2,0:T(8,128)S(1)}, f32[2,8,3,64]{3,1,2,0:T(8,128)}, u32[]{:S(2)}) copy-start(f32[2,8,3,64]{3,1,2,0:T(8,128)} %param.12) | copy-start | bytes 36868
  4.9 0.7 %copy-start.6 = (bf16[2,64]{1,0:T(2,128)(2,1)S(1)}, bf16[2,64]{1,0:T(2,128)(2,1)}, u32[]{:S(2)}) copy-start(bf16[2,64]{1,0:T(2,128)(2,1)} %param.16) | copy-start | bytes 772
  4.9 0.9 %copy-start.1 = (bf16[2,12,6,256]{3,0,2,1:T(2,128)(2,1)S(1)}, bf16[2,12,6,256]{3,0,2,1:T(2,128)(2,1)}, u32[]{:S(2)}) copy-start(bf16[2,12,6,256]{3,0,2,1:T(2,128)(2,1)} %param.10) | copy-start | bytes 221188
  5.8 1.0 %copy-start = (bf16[2,3,3,64,64]{4,3,2,1,0:T(8,128)(2,1)S(1)}, bf16[2,3,3,64,64]{4,3,2,1,0:T(8,128)(2,1)}, u32[]{:S(2)}) copy-start(bf16[2,3,3,64,64]{4,3,2,1,0:T(8,128)(2,1)} %param.15) | copy-start | bytes 442372

commit v3 on v2

--- a/solution.py
+++ b/solution.py
@@ -14,14 +14,6 @@
 LC = 4
 
 
-def real_block(weights):
-    real_part = weights[0]
-    imag_part = weights[1]
-    upper = jnp.concatenate([real_part, imag_part], axis=-1)
-    lower = jnp.concatenate([-imag_part, real_part], axis=-1)
-    return jnp.concatenate([upper, lower], axis=-2)
-
-
 def mm(a, b):
     return jnp.dot(a, b, preferred_element_type=jnp.float32)
 
@@ -32,9 +24,10 @@
 
 def step_kernel(
     dims, scale,
-    slc_ref, pick_ref, avg_ref, tgt_ref, w1_ref, wf_ref, bm_ref, wp_ref, wpb_ref, wb_ref,
+    slc_ref, pick_ref, avg_ref, tgt_ref, wl_any, bl_any, wmid_any, bmid_any, wproj_any,
     den_ref, o_ref, small_ref,
     pool, look_f, look_s, look_r, tgt_r, fld, tfld, i3a, i3b, h2s, tsum, dn3, dnm3, dp2m, dp1, outs, x_ref,
+    wl_in, bl_in, wm_in, bm_in, wj_in, w_sem, w1_ref, wp_ref, wpb_ref, wf_ref, wb_ref, bm_ref, wtmp,
     plane_in, date_in, small_in, small_date, small_sem, small_date_sem, slab_sem, look_sem, tgt_sem, den_sem, plane_sem, date_sem, gather_sem,
 ):
     n_row, n_col, n_date, pp, tr, tc = dims
@@ -64,6 +57,12 @@
         copy.start()
         return copy
 
+    fetches = []
+    wide = zip((wl_any, bl_any, wmid_any, bmid_any, wproj_any), (wl_in, bl_in, wm_in, bm_in, wj_in))
+    for k, (src, dst) in enumerate(wide):
+        copy = pltpu.make_async_copy(src, dst, w_sem.at[k])
+        copy.start()
+        fetches.append(copy)
     barrier = pltpu.get_barrier_semaphore()
     for k in range(1, n_plane):
         pl.semaphore_signal(barrier, inc=1, device_id=plane_peer(k)[1], device_id_type=MESH)
@@ -101,6 +100,38 @@
     spot = c * tc + lane - base
     inside = (spot >= 0) & (spot < n_col * tc)
     own = (lane >= base) & (lane < base + tc)
+    for copy in fetches:
+        copy.wait()
+    wtmp[...] = jnp.zeros_like(wtmp)
+
+    def joined(a, b):
+        return jnp.concatenate([a, b], axis=1)
+
+    for t in range(3):
+        for u in range(3):
+            pair = wl_in[t, u].astype(f32)
+            at = 8 * t + 2 * u
+            wtmp[0, at : at + 1, :] = joined(pair[0:1], pair[1:2])
+            wtmp[0, at + 1 : at + 2, :] = joined(-pair[1:2], pair[0:1])
+            pair = wj_in[t, u].astype(f32)
+            real, imag = joined(pair[0:1], -pair[1:2]), joined(pair[1:2], pair[0:1])
+            flip = 8 * (2 - t) + 2 * (2 - u)
+            wtmp[1, at : at + 1, :] = real
+            wtmp[1, at + 1 : at + 2, :] = imag
+            wtmp[2, flip : flip + 1, :] = real
+            wtmp[2, flip + 1 : flip + 2, :] = imag
+            wr, wi = wm_in[0, t, u].astype(f32), wm_in[1, t, u].astype(f32)
+            block = jnp.concatenate([joined(wr, wi), joined(-wi, wr)], axis=0)
+            wb_ref[2 - t, :, (2 - u) * 128 : (3 - u) * 128] = block.astype(bf16)
+            wf_ref[t, :, u * 128 : (u + 1) * 128] = block.T.astype(bf16)
+    bias = bl_in[...].astype(f32)
+    wtmp[0, 14:15, :] = joined(bias[0:1], bias[1:2])
+    bias = bm_in[...].astype(f32)
+    wtmp[3, 0:1, :] = joined(bias[0:1], bias[1:2])
+    w1_ref[...] = wtmp[0].T[:, 0:32].astype(bf16)
+    wp_ref[...] = wtmp[1, 0:32].astype(bf16)
+    wpb_ref[...] = wtmp[2].T[:, 0:32].astype(bf16)
+    bm_ref[...] = wtmp[3].T[:, 0:1]
     for copy in slabs:
         copy.wait_recv()
     sent += slabs
@@ -346,23 +377,7 @@
     avg = jnp.where(spots == jnp.arange(128, dtype=jnp.int32)[None, :], 1.0 / (LR * LC), 0.0).astype(f32)
     tgt = target.reshape(2, n_row, pp, tr, tc).transpose(1, 0, 3, 2, 4).reshape(n_row, rows, tc)
     tgt = jnp.pad(tgt, ((0, 0), (0, pad_rows - rows), (0, 128 - tc)))
-    lift = real_block(w_lift[:, :, :, None, :])
-    lift = jnp.pad(lift.reshape(3, 6, 2 * ch), ((0, 0), (0, 2), (0, 0)))
-    lift = lift.at[1, 6].set(b_lift.reshape(2 * ch))
-    w1 = jnp.pad(lift.reshape(24, 2 * ch), ((0, 8), (0, 0))).T
-    mid = real_block(w_mid)
-    wf = mid.reshape(3, 6 * ch, 2 * ch).transpose(0, 2, 1)
-    wb = mid[::-1, ::-1].transpose(0, 2, 1, 3).reshape(3, 2 * ch, 6 * ch)
-    proj = real_block(w_proj[..., None])
-
-    def tap_rows(kernel):
-        kernel = kernel.transpose(0, 1, 3, 2).reshape(3, 6, 2 * ch)
-        kernel = jnp.pad(kernel, ((0, 0), (0, 2), (0, 0))).reshape(24, 2 * ch)
-        return jnp.pad(kernel, ((0, 8), (0, 0)))
-
-    wp = tap_rows(proj)
-    wpb = tap_rows(proj[::-1, ::-1]).T
-    bm = b_mid.reshape(2 * ch, 1).astype(f32)
+    w_lift, w_proj = w_lift.transpose(1, 2, 0, 3), w_proj.transpose(1, 2, 0, 3)
     scale = 1.0 / math.sqrt(2.0 * count * n_date * tr * n_row * tc * n_col)
     nb = (n_row * tr + 1) * pp
     n, wide = nb * 128, (nb + 2) * 128
@@ -377,7 +392,7 @@
             jax.ShapeDtypeStruct((n_plane * piece, 128), f32),
             jax.ShapeDtypeStruct((24, 128), f32),
         ),
-        in_specs=[pl.BlockSpec(memory_space=vmem)] * 10,
+        in_specs=[pl.BlockSpec(memory_space=vmem)] * 4 + [pl.BlockSpec(memory_space=pl.ANY)] * 5,
         out_specs=(pl.BlockSpec(memory_space=vmem),) * 3,
         scratch_shapes=[
             vmem((2,) + packed.shape, bf16),
@@ -397,6 +412,19 @@
             vmem((2 * ch, n), bf16),
             vmem((n_row, pad_rows, 128), f32),
             vmem((n_plane * piece, 128), f32),
+            vmem(w_lift.shape, bf16),
+            vmem(b_lift.shape, bf16),
+            vmem(w_mid.shape, bf16),
+            vmem(b_mid.shape, bf16),
+            vmem(w_proj.shape, bf16),
+            dma((5,)),
+            vmem((2 * ch, 32), bf16),
+            vmem((32, 2 * ch), bf16),
+            vmem((2 * ch, 32), bf16),
+            vmem((3, 2 * ch, 6 * ch), bf16),
+            vmem((3, 2 * ch, 6 * ch), bf16),
+            vmem((2 * ch, 1), f32),
+            vmem((4, 128, 128), f32),
             vmem((n_plane, piece, 128), f32),
             vmem((n_date, piece, 128), f32),
             vmem((n_plane, 24, 128), f32),
@@ -414,7 +442,7 @@
         compiler_params=pltpu.CompilerParams(
             collective_id=0, has_side_effects=True, vmem_limit_bytes=48 * 1024 * 1024
         ),
-    )(packed, pick, avg, tgt, w1, wf, bm, wp, wpb, wb)
+    )(packed, pick, avg, tgt, w_lift, b_lift, w_mid, b_mid, w_proj)
     denoised = den[:, :rows, :tc].reshape(n_row, 2, tr, pp, tc).transpose(1, 0, 3, 2, 4)
     denoised = denoised.reshape(2, count, tr, tc)
     grad_mid = sums[: 9 * ch].reshape(3, 3, ch, 2, ch).transpose(3, 0, 1, 2, 4)

time: 52.8 us -> 47.8 us (0.905)
  local copies, waits for them, and re-layouts: 9.6 us -> 5.09 us
    unnamed x20 -> x16, local copies, waits for them, and re-layouts: 4.67 us -> 1.53 us
    reshape x9 -> x0, local copies, waits for them, and re-layouts: 0.76 us -> none  [the longest x1 0.22 us: local(): wb = mid[::-1, ::-1].transpose(0, 2, 1, 3).reshape(3, 2 * ch, 6 * ch)]
    mul x1, other arithmetic: 0.01 us -> 0.68 us  [local(): index[:, None, :] * kinds]
    another operation x1 -> x0, other arithmetic: 0.61 us -> none  [local(): jnp.stack([g_proj[:, :, 0, 0] + g_proj[:, :, 1, 1], g_proj[:, :, 1, 0] -...]
where the time goes in v3:
time: 47.8 us; the launch traced here: 47.6 us
  Pallas kernels  40.1 us (84%)
  local copies, waits for them, and re-layouts  5.09 us (11%)
  other arithmetic  1.53 us (3%)
  between operations  0.81 us (2%)
    pallas_call x1, Pallas kernels, local(): pl.pallas_call(functools.partial(step_kernel, (n_row, n_col, n_date, pp,...  40.1 us
    unnamed x16, local copies, waits for them, and re-layouts  1.53 us
    reshape x2, local copies, waits for them, and re-layouts, local(): grad_mid = sums[:9 * ch].reshape(3, 3, ch, 2, ch).transpose(3, 0, 1, 2, 4)  1.24 us

profile of v3, /device:TPU:1, one launch (start us, length us, event | category | flops | bytes accessed | tf_op | source)
XLA Modules:
  0.0 47.6 jit_solution(6643668521886904679)
XLA Ops:
  0.6 0.0 copy-start.6
  0.6 0.7 %multiply_bitcast_fusion = s32[2,8]{1,0:T(2,128)S(1)} fusion(s32[8,2]{0,1:T(2,128)} %param.9, s32[]{:T(128)S(6)} %mul.10), kind=kLoop, calls=%fused_computation.24 | loop fusion | flops 32 | bytes 132 | tf_op jit(solution)/shard_map/mul | solution.py:374
  1.3 0.1 add.57
  1.4 0.0 copy-done.6
  1.4 0.0 copy-start.5
  1.5 0.1 fusion.1.pick_ref
  1.6 0.8 %copy-done.5 = bf16[2,12,6,256]{3,0,2,1:T(2,128)(2,1)S(1)} copy-done((bf16[2,12,6,256]{3,0,2,1:T(2,128)(2,1)S(1)}, bf16[2,12,6,256]{3,0,2,1:T(2,128)(2,1)}, u32[]{:S(2)}) %copy-start.5) | copy-done | bytes 73752
  2.3 0.0 copy-start
  2.3 0.1 reshape.170
  2.4 0.0 copy-start.1
  2.4 0.0 copy-start.2
  2.5 0.0 copy-start.3
  2.5 0.0 copy-start.4
  2.5 0.1 fusion.avg_ref
  2.6 0.7 %copy-done = bf16[2,3,3,64,64]{4,3,2,1,0:T(8,128)(2,1)S(1)} copy-done((bf16[2,3,3,64,64]{4,3,2,1,0:T(8,128)(2,1)S(1)}, bf16[2,3,3,64,64]{4,3,2,1,0:T(8,128)(2,1)}, u32[]{:S(2)}) %copy-start) | copy-done | bytes 147480
  3.3 0.0 copy-done.1
  3.3 0.0 copy-done.2
  3.3 0.0 copy-done.3
  3.3 0.0 copy-done.4
  3.3 40.1 %shard_map.127 = (f32[4,16,128]{2,1,0:T(8,128)S(1)}, f32[640,128]{1,0:T(8,128)S(1)}, f32[24,128]{1,0:T(8,128)S(1)}) custom-call(bf16[48,768]{1,0:T(8,128)(2,1)S(1)} %bitcast.51, bf16[64,144]{1,0:T(8,128)(2,1)S(1)} %fusion.1.pick_ref, f32[256,128]{1,0:T(8,128)S(1)} %fusion.avg_ref, f32[4,16,128]{2,1,0:T(8,128)S(1)} %pad.4.tgt_ref, ...), custom_call_target="tpu_custom_call" | custom-call | tf_op jit(solution)/shard_map/pallas_call | solution.py:388
  43.5 0.6 %copy.31 = f32[2,4,2,3,64]{4,2,1,3,0:T(2,128)} copy(f32[2,4,2,3,64]{4,1,2,3,0:T(4,128)S(1)} %bitcast.59) | data formatting | bytes 24576 | tf_op jit(solution)/shard_map/transpose | solution.py:446
  44.1 0.6 %reshape_squeeze.6 = f32[2,64]{1,0:T(2,128)} reshape(f32[128]{0:T(128)S(1)} %slice_reduce_fusion) | data formatting | bytes 1024 | tf_op jit(solution)/shard_map/reshape;squeeze | solution.py:462
  44.8 0.6 %reshape_squeeze.7 = f32[2,64]{1,0:T(2,128)} reshape(f32[128]{0:T(128)S(1)} %slice_reduce_fusion.1) | data formatting | bytes 1024 | tf_op jit(solution)/shard_map/reshape;squeeze | solution.py:464
  45.4 0.1 reshape.180
  45.6 0.1 reshape.177
  45.7 0.6 %pad_maximum_fusion = (f32[2,3,3,64]{3,0,2,1:T(2,128)}, f32[2,3,3,64]{3,0,2,1:T(2,128)}) fusion(f32[1,3,3,64]{3,0,2,1:T(1,128)S(1)} %fusion.2, f32[1,3,3,64]{3,0,2,1:T(1,128)S(1)} %fusion.4, f32[1,3,3,64]{3,0,2,1:T(1,128)S(1)} %subtract_bitcast_fusion, f32[1,3,3,64]{3,0,2,1:T(1,128)S(1)} %add_bitcast_fusion), kind=kLoop, calls=%fused_computation.7 | loop fusion | flops 2304 | bytes 18432 | tf_op jit(solution)/shard_map/stack | solution.py:452
  46.3 0.4 reshape.178
  46.7 0.9 %copy.44 = f32[3,3,64,2,64]{4,2,1,0,3:T(8,128)} copy(f32[3,3,64,2,64]{4,3,2,1,0:T(2,128)S(1)} %reshape.178) | data formatting | bytes 589824 | tf_op jit(solution)/shard_map/reshape | solution.py:448
  (17 shorter events, 0.2 us)
Async XLA Ops:
  0.6 0.8 %copy-start.6 = (f32[2,8,3,64]{3,1,2,0:T(8,128)S(1)}, f32[2,8,3,64]{3,1,2,0:T(8,128)}, u32[]{:S(2)}) copy-start(f32[2,8,3,64]{3,1,2,0:T(8,128)} %param.10) | copy-start | bytes 36868
  1.4 0.9 %copy-start.5 = (bf16[2,12,6,256]{3,0,2,1:T(2,128)(2,1)S(1)}, bf16[2,12,6,256]{3,0,2,1:T(2,128)(2,1)}, u32[]{:S(2)}) copy-start(bf16[2,12,6,256]{3,0,2,1:T(2,128)(2,1)} %param.8) | copy-start | bytes 221188
  2.3 1.0 %copy-start = (bf16[2,3,3,64,64]{4,3,2,1,0:T(8,128)(2,1)S(1)}, bf16[2,3,3,64,64]{4,3,2,1,0:T(8,128)(2,1)}, u32[]{:S(2)}) copy-start(bf16[2,3,3,64,64]{4,3,2,1,0:T(8,128)(2,1)} %wmid_any.1) | copy-start | bytes 442372
  2.4 0.9 %copy-start.1 = (bf16[2,3,3,64]{3,0,2,1:T(2,128)(2,1)S(1)}, bf16[2,3,3,64]{3,0,2,1:T(2,128)(2,1)}, u32[]{:S(2)}) copy-start(bf16[2,3,3,64]{3,0,2,1:T(2,128)(2,1)} %param.11) | copy-start | bytes 6916
  2.4 0.8 %copy-start.2 = (bf16[2,3,3,64]{3,0,2,1:T(2,128)(2,1)S(1)}, bf16[2,3,3,64]{3,0,2,1:T(2,128)(2,1)}, u32[]{:S(2)}) copy-start(bf16[2,3,3,64]{3,0,2,1:T(2,128)(2,1)} %param.15) | copy-start | bytes 6916
  2.5 0.8 %copy-start.3 = (bf16[2,64]{1,0:T(2,128)(2,1)S(1)}, bf16[2,64]{1,0:T(2,128)(2,1)}, u32[]{:S(2)}) copy-start(bf16[2,64]{1,0:T(2,128)(2,1)} %bl_any.1) | copy-start | bytes 772
  2.5 0.8 %copy-start.4 = (bf16[2,64]{1,0:T(2,128)(2,1)S(1)}, bf16[2,64]{1,0:T(2,128)(2,1)}, u32[]{:S(2)}) copy-start(bf16[2,64]{1,0:T(2,128)(2,1)} %bmid_any.1) | copy-start | bytes 772

commit v4 on v3

--- a/solution.py
+++ b/solution.py
@@ -355,6 +355,31 @@
         copy.wait_recv()
     for copy in sent + scatter + small + spread + small_spread + gather:
         copy.wait_send()
+
+
+def finish_kernel(dims, den, sums, small, den_out, lift_out, lbias_out, mid_out, mbias_out, proj_out):
+    n_row, pp, tr, tc, ch = dims
+    for k in range(n_row):
+        for z in range(2):
+            for t in range(tr):
+                at = (z * tr + t) * pp
+                den_out[z, t, k * pp : (k + 1) * pp, :] = den[k, at : at + pp, 0:tc]
+    for t in range(3):
+        for u in range(3):
+            at = 8 * t + 2 * u
+            upper, lower = small[at : at + 1, :], small[at + 1 : at + 2, :]
+            lift_out[t, u, 0:1, :] = upper[:, 0:ch] + lower[:, ch:]
+            lift_out[t, u, 1:2, :] = upper[:, ch:] - lower[:, 0:ch]
+            at = 576 + 8 * (2 - t) + 2 * (2 - u)
+            upper, lower = sums[at : at + 1, :], sums[at + 1 : at + 2, :]
+            proj_out[t, u, 0:1, :] = upper[:, 0:ch] + lower[:, ch:]
+            proj_out[t, u, 1:2, :] = lower[:, 0:ch] - upper[:, ch:]
+            at = (3 * t + u) * ch
+            for z in range(2):
+                mid_out[z, t, u] = sums[at : at + ch, z * ch : (z + 1) * ch]
+    for z in range(2):
+        lbias_out[z : z + 1, :] = small[14:15, z * ch : (z + 1) * ch]
+        mbias_out[z : z + 1, :] = sums[600:601, z * ch : (z + 1) * ch]
 
 
 def local(slc, pairs, target, w_lift, b_lift, w_mid, b_mid, w_proj):
@@ -443,26 +468,28 @@
             collective_id=0, has_side_effects=True, vmem_limit_bytes=48 * 1024 * 1024
         ),
     )(packed, pick, avg, tgt, w_lift, b_lift, w_mid, b_mid, w_proj)
-    denoised = den[:, :rows, :tc].reshape(n_row, 2, tr, pp, tc).transpose(1, 0, 3, 2, 4)
-    denoised = denoised.reshape(2, count, tr, tc)
-    grad_mid = sums[: 9 * ch].reshape(3, 3, ch, 2, ch).transpose(3, 0, 1, 2, 4)
-    g_lift = small.reshape(3, 8, 2 * ch)
-    lift_bias = g_lift[1, 6]
-    g_lift = g_lift[:, :6].reshape(3, 3, 2, 2, ch)
-    grad_lift = jnp.stack(
-        [g_lift[:, :, 0, 0] + g_lift[:, :, 1, 1], g_lift[:, :, 0, 1] - g_lift[:, :, 1, 0]]
-    )
-    g_proj = sums[576:600].reshape(3, 8, 2 * ch)[:, :6].reshape(3, 3, 2, 2, ch)[::-1, ::-1]
-    grad_proj = jnp.stack(
-        [g_proj[:, :, 0, 0] + g_proj[:, :, 1, 1], g_proj[:, :, 1, 0] - g_proj[:, :, 0, 1]]
-    )
+    shape = jax.ShapeDtypeStruct
+    denoised, grad_lift, lift_bias, grad_mid, mid_bias, grad_proj = pl.pallas_call(
+        functools.partial(finish_kernel, (n_row, pp, tr, tc, ch)),
+        out_shape=(
+            shape((2, tr, count, tc), f32),
+            shape((3, 3, 2, ch), f32),
+            shape((2, ch), f32),
+            shape((2, 3, 3, ch, ch), f32),
+            shape((2, ch), f32),
+            shape((3, 3, 2, ch), f32),
+        ),
+        in_specs=[pl.BlockSpec(memory_space=vmem)] * 3,
+        out_specs=(pl.BlockSpec(memory_space=vmem),) * 6,
+        compiler_params=pltpu.CompilerParams(vmem_limit_bytes=8 * 1024 * 1024),
+    )(den, sums, small)
     return (
-        denoised,
-        grad_lift,
-        lift_bias.reshape(2, ch),
+        denoised.transpose(0, 2, 1, 3),
+        grad_lift.transpose(2, 0, 1, 3),
+        lift_bias,
         grad_mid,
-        sums[600].reshape(2, ch),
-        grad_proj,
+        mid_bias,
+        grad_proj.transpose(2, 0, 1, 3),
     )
 
 

time: 47.8 us -> 44.7 us (0.935)
  local copies, waits for them, and re-layouts: 5.09 us -> 1.69 us
  Pallas kernels: 40.1 us -> 41.2 us
  other arithmetic: 1.53 us -> 0.87 us
    reshape x5 -> x0, local copies, waits for them, and re-layouts: 1.4 us -> none  [the longest x2 1.24 us: local(): grad_mid = sums[:9 * ch].reshape(3, 3, ch, 2, ch).transpose(3, 0, 1, 2, 4)]
    another operation x2 -> x0, local copies, waits for them, and re-layouts: 1.29 us -> none  [the longest x1 0.64 us: local(): lift_bias.reshape(2, ch)]
    pallas_call x0 -> x1, Pallas kernels: none -> 1.05 us  [local(): pl.pallas_call(functools.partial(finish_kernel, (n_row, pp, tr, tc, ch)),...]
    another operation x1 -> x0, other arithmetic: 0.63 us -> none  [local(): jnp.stack([g_lift[:, :, 0, 0] + g_lift[:, :, 1, 1], g_lift[:, :, 0, 1] -...]
    transpose x1 -> x0, local copies, waits for them, and re-layouts: 0.62 us -> none  [local(): den[:, :rows, :tc].reshape(n_row, 2, tr, pp, tc).transpose(1, 0, 3, 2, 4)]
    unnamed x16 -> x15, local copies, waits for them, and re-layouts: 1.53 us -> 1.51 us
where the time goes in v4:
time: 44.7 us; the launch traced here: 44.5 us
  Pallas kernels  41.2 us (92%)
  local copies, waits for them, and re-layouts  1.69 us (4%)
  other arithmetic  0.87 us (2%)
  between operations  0.76 us (2%)
    pallas_call x1, Pallas kernels, local(): pl.pallas_call(functools.partial(step_kernel, (n_row, n_col, n_date, pp,...  40.1 us
    unnamed x15, local copies, waits for them, and re-layouts  1.51 us
    pallas_call x1, Pallas kernels, local(): pl.pallas_call(functools.partial(finish_kernel, (n_row, pp, tr, tc, ch)),...  1.05 us

profile of v4, /device:TPU:1, one launch (start us, length us, event | category | flops | bytes accessed | tf_op | source)
XLA Modules:
  0.0 44.5 jit_solution(1927783430298262876)
XLA Ops:
  0.6 0.0 copy-start.6
  0.6 0.7 %multiply_bitcast_fusion = s32[2,8]{1,0:T(2,128)S(1)} fusion(s32[8,2]{0,1:T(2,128)} %param.9, s32[]{:T(128)S(6)} %mul.10), kind=kLoop, calls=%fused_computation.10 | loop fusion | flops 32 | bytes 132 | tf_op jit(solution)/shard_map/mul | solution.py:399
  1.3 0.1 add.31
  1.4 0.0 copy-done.6
  1.4 0.0 copy-start.5
  1.5 0.1 fusion.1.pick_ref
  1.6 0.8 %copy-done.5 = bf16[2,12,6,256]{3,0,2,1:T(2,128)(2,1)S(1)} copy-done((bf16[2,12,6,256]{3,0,2,1:T(2,128)(2,1)S(1)}, bf16[2,12,6,256]{3,0,2,1:T(2,128)(2,1)}, u32[]{:S(2)}) %copy-start.5) | copy-done | bytes 73752
  2.3 0.0 copy-start
  2.3 0.1 reshape.77
  2.4 0.0 copy-start.1
  2.4 0.0 copy-start.2
  2.5 0.0 copy-start.3
  2.5 0.0 copy-start.4
  2.5 0.1 fusion.avg_ref
  2.6 0.7 %copy-done = bf16[2,3,3,64,64]{4,3,2,1,0:T(8,128)(2,1)S(1)} copy-done((bf16[2,3,3,64,64]{4,3,2,1,0:T(8,128)(2,1)S(1)}, bf16[2,3,3,64,64]{4,3,2,1,0:T(8,128)(2,1)}, u32[]{:S(2)}) %copy-start) | copy-done | bytes 147480
  3.3 0.0 copy-done.1
  3.3 0.0 copy-done.2
  3.3 0.0 copy-done.3
  3.3 0.0 copy-done.4
  3.3 40.1 %shard_map.127 = (f32[4,16,128]{2,1,0:T(8,128)S(1)}, f32[640,128]{1,0:T(8,128)S(1)}, f32[24,128]{1,0:T(8,128)S(1)}) custom-call(bf16[48,768]{1,0:T(8,128)(2,1)S(1)} %bitcast.19, bf16[64,144]{1,0:T(8,128)(2,1)S(1)} %fusion.1.pick_ref, f32[256,128]{1,0:T(8,128)S(1)} %fusion.avg_ref, f32[4,16,128]{2,1,0:T(8,128)S(1)} %pad.4.tgt_ref, ...), custom_call_target="tpu_custom_call" | custom-call | tf_op jit(solution)/shard_map/pallas_call | solution.py:413
  43.4 1.0 %shard_map.128 = (f32[2,3,8,64]{3,2,1,0:T(8,128)}, f32[3,3,2,64]{3,2,1,0:T(2,128)}, f32[2,64]{1,0:T(2,128)}, f32[2,3,3,64,64]{4,3,2,1,0:T(8,128)}, f32[2,64]{1,0:T(2,128)}, /*index=5*/f32[3,3,2,64]{3,2,1,0:T(2,128)}) custom-call(f32[4,16,128]{2,1,0:T(8,128)S(1)} %get-tuple-element.15.den, f32[640,128]{1,0:T(8,128)S(1)} %get-tuple-element.16.sums, ...), custom_call_target="tpu_custom_call" | custom-call | tf_op jit(solution)/shard_map/pallas_call | solution.py:472
  (7 shorter events, 0.1 us)
Async XLA Ops:
  0.6 0.8 %copy-start.6 = (f32[2,8,3,64]{3,1,2,0:T(8,128)S(1)}, f32[2,8,3,64]{3,1,2,0:T(8,128)}, u32[]{:S(2)}) copy-start(f32[2,8,3,64]{3,1,2,0:T(8,128)} %param.10) | copy-start | bytes 36868
  1.4 0.9 %copy-start.5 = (bf16[2,12,6,256]{3,0,2,1:T(2,128)(2,1)S(1)}, bf16[2,12,6,256]{3,0,2,1:T(2,128)(2,1)}, u32[]{:S(2)}) copy-start(bf16[2,12,6,256]{3,0,2,1:T(2,128)(2,1)} %param.8) | copy-start | bytes 221188
  2.3 1.0 %copy-start = (bf16[2,3,3,64,64]{4,3,2,1,0:T(8,128)(2,1)S(1)}, bf16[2,3,3,64,64]{4,3,2,1,0:T(8,128)(2,1)}, u32[]{:S(2)}) copy-start(bf16[2,3,3,64,64]{4,3,2,1,0:T(8,128)(2,1)} %wmid_any.1) | copy-start | bytes 442372
  2.4 0.9 %copy-start.1 = (bf16[2,3,3,64]{3,0,2,1:T(2,128)(2,1)S(1)}, bf16[2,3,3,64]{3,0,2,1:T(2,128)(2,1)}, u32[]{:S(2)}) copy-start(bf16[2,3,3,64]{3,0,2,1:T(2,128)(2,1)} %param.11) | copy-start | bytes 6916
  2.4 0.8 %copy-start.2 = (bf16[2,3,3,64]{3,0,2,1:T(2,128)(2,1)S(1)}, bf16[2,3,3,64]{3,0,2,1:T(2,128)(2,1)}, u32[]{:S(2)}) copy-start(bf16[2,3,3,64]{3,0,2,1:T(2,128)(2,1)} %param.15) | copy-start | bytes 6916
  2.5 0.8 %copy-start.3 = (bf16[2,64]{1,0:T(2,128)(2,1)S(1)}, bf16[2,64]{1,0:T(2,128)(2,1)}, u32[]{:S(2)}) copy-start(bf16[2,64]{1,0:T(2,128)(2,1)} %bl_any.1) | copy-start | bytes 772
  2.5 0.8 %copy-start.4 = (bf16[2,64]{1,0:T(2,128)(2,1)S(1)}, bf16[2,64]{1,0:T(2,128)(2,1)}, u32[]{:S(2)}) copy-start(bf16[2,64]{1,0:T(2,128)(2,1)} %bmid_any.1) | copy-start | bytes 772
